TPU v7x, 32 devices: a whole 2x2x4 slice. The times are simulated.
32 devices in a mesh: grp: 2 (over y), seq: 4 (over z), ch: 4 (over x, core).
Axes of the slice: x: 2, y: 2, z: 4, core: 2. Of those that a mesh axis runs over, the one named last changes fastest.
Arguments:
- activations: bfloat16 [4096, 1024], P('ch', ('grp', 'seq')), parts along dimension 1, may hold values from -6 to 6
- projection: bfloat16 [4096, 2048], P('seq', 'ch'), may hold values from -0.09375 to 0.09375
- medium_taps: float32 [2048, 128], P('ch'), may hold values from -0.5 to 0.5
- long_filters: bfloat16 [2048, 512], P('ch', 'seq'), may hold values from -0.25 to 0.25
- cotangent: bfloat16 [2048, 1024], P('ch', ('grp', 'seq')), parts along dimension 1, may hold values from -6 to 6
Outputs:
- conv_out: bfloat16 [2048, 1024], P('ch', ('grp', 'seq')), parts along dimension 1
- input_grad: bfloat16 [4096, 1024], P('ch', ('grp', 'seq')), parts along dimension 1
There are 2 independent parts, one for each index of `grp`. A program takes and returns all parts, laid end to end along the dimension named above; an argument that names none is the same for every part. Nothing has to cross between parts.
All inputs are finite; a program needn't handle non-finite values.
Results may differ from a plain program's by a relative error of at most 0.012.
Values may be sent and summed in bfloat16 or wider, within the bound.
A program may use at most 64 MiB of HBM per device.

v0:
```python
import math

import jax
import jax.numpy as jnp
from jax import lax
from jax.sharding import PartitionSpec as P

exact_mode = lax.Precision.HIGH


def medium_forward(padded, tap_weights, length):
    tap_count = tap_weights.shape[1]
    summed = jnp.zeros((padded.shape[0], length), jnp.float32)
    for offset in range(tap_count):
        begin_col = tap_count - 1 - offset
        summed = (
            summed + tap_weights[:, offset : offset + 1] * padded[:, begin_col : begin_col + length]
        )
    return summed


def medium_backward(padded, tap_weights, length):
    tap_count = tap_weights.shape[1]
    summed = jnp.zeros((padded.shape[0], length), jnp.float32)
    for offset in range(tap_count):
        summed = summed + tap_weights[:, offset : offset + 1] * padded[:, offset : offset + length]
    return summed


def dft_tables(length):
    points = 2 * length
    columns = 128
    row_count = points // columns
    half_rows = row_count // 2
    freq_rows = jnp.arange(row_count, dtype=jnp.int32)
    time_rows = jnp.arange(half_rows, dtype=jnp.int32)
    lane_index = jnp.arange(columns, dtype=jnp.int32)
    angle_first = (
        2.0
        * math.pi
        / row_count
        * (freq_rows[:, None] * time_rows[None, :] % row_count).astype(jnp.float32)
    )
    angle_twist = (
        2.0
        * math.pi
        / points
        * (freq_rows[:, None] * lane_index[None, :] % points).astype(jnp.float32)
    )
    angle_last = (
        2.0
        * math.pi
        / columns
        * (lane_index[:, None] * lane_index[None, :] % columns).astype(jnp.float32)
    )
    return (
        jnp.cos(angle_first),
        jnp.sin(angle_first),
        jnp.cos(angle_twist),
        jnp.sin(angle_twist),
        jnp.cos(angle_last),
        jnp.sin(angle_last),
    )


def forward_dft(signal, tables):
    cos_first, sin_first, cos_twist, sin_twist, cos_last, sin_last = tables
    channels = signal.shape[0]
    shaped = signal.reshape(channels, cos_first.shape[1], 128)
    section_re = jnp.einsum("kn,cnq->ckq", cos_first, shaped, precision=exact_mode)
    section_im = -jnp.einsum("kn,cnq->ckq", sin_first, shaped, precision=exact_mode)
    twist_re = section_re * cos_twist + section_im * sin_twist
    twist_im = section_im * cos_twist - section_re * sin_twist
    spec_re = jnp.einsum("ckq,qm->ckm", twist_re, cos_last, precision=exact_mode) + jnp.einsum(
        "ckq,qm->ckm", twist_im, sin_last, precision=exact_mode
    )
    spec_im = jnp.einsum("ckq,qm->ckm", twist_im, cos_last, precision=exact_mode) - jnp.einsum(
        "ckq,qm->ckm", twist_re, sin_last, precision=exact_mode
    )
    return (spec_re, spec_im)


def inverse_dft(spec_re, spec_im, tables):
    cos_first, sin_first, cos_twist, sin_twist, cos_last, sin_last = tables
    channels = spec_re.shape[0]
    half_rows = cos_first.shape[1]
    inner_re = jnp.einsum("ckq,qm->ckm", spec_re, cos_last, precision=exact_mode) - jnp.einsum(
        "ckq,qm->ckm", spec_im, sin_last, precision=exact_mode
    )
    inner_im = jnp.einsum("ckq,qm->ckm", spec_im, cos_last, precision=exact_mode) + jnp.einsum(
        "ckq,qm->ckm", spec_re, sin_last, precision=exact_mode
    )
    turned_re = inner_re * cos_twist - inner_im * sin_twist
    turned_im = inner_im * cos_twist + inner_re * sin_twist
    output = jnp.einsum("kn,ckq->cnq", cos_first, turned_re, precision=exact_mode) - jnp.einsum(
        "kn,ckq->cnq", sin_first, turned_im, precision=exact_mode
    )
    points = 2 * half_rows * 128
    return (output / points).reshape(channels, half_rows * 128)


def causal_apply(signal, filt_re, filt_im, tables, conjugate):
    sig_re, sig_im = forward_dft(signal, tables)
    if conjugate:
        prod_re = sig_re * filt_re + sig_im * filt_im
        prod_im = sig_im * filt_re - sig_re * filt_im
    else:
        prod_re = sig_re * filt_re - sig_im * filt_im
        prod_im = sig_im * filt_re + sig_re * filt_im
    return inverse_dft(prod_re, prod_im, tables)


def on_device(activations, projection, medium_taps, long_filters, cotangent):
    tap_count = medium_taps.shape[1]
    whole_in = lax.all_gather(activations, "ch", axis=0, tiled=True)
    mixed_sum = lax.dot_general(
        lax.all_gather(projection, "seq", axis=0, tiled=True),
        whole_in,
        (((0,), (0,)), ((), ())),
        preferred_element_type=jnp.float32,
    )
    values = mixed_sum.astype(jnp.bfloat16)
    channel_count = values.shape[0] // lax.axis_size("seq")
    own_taps = lax.dynamic_slice_in_dim(
        medium_taps, lax.axis_index("seq") * channel_count, channel_count, 0
    )
    arrived, filters_ch = (
        lax.all_to_all(values, "seq", split_axis=0, concat_axis=1, tiled=True),
        lax.all_to_all(long_filters, "seq", split_axis=0, concat_axis=1, tiled=True),
    )
    tables = dft_tables(arrived.shape[1])
    filt_re, filt_im = forward_dft(filters_ch.astype(jnp.float32), tables)
    values_ch = arrived.astype(jnp.float32)
    padded_ch = jnp.pad(values_ch, ((0, 0), (tap_count - 1, 0)))
    conv_ch = medium_forward(padded_ch, own_taps, arrived.shape[1])
    gate_ch = jax.nn.sigmoid(values_ch)
    signal = lax.optimization_barrier((conv_ch * gate_ch).astype(jnp.bfloat16)).astype(jnp.float32)
    kept_state = (conv_ch, gate_ch)
    output_ch = causal_apply(signal, filt_re, filt_im, tables, False).astype(jnp.bfloat16)
    output_ch, context = (output_ch, (filt_re, filt_im, tables, kept_state))
    conv_out = lax.all_to_all(output_ch, "seq", split_axis=1, concat_axis=0, tiled=True)
    grad_ch = lax.all_to_all(cotangent, "seq", split_axis=0, concat_axis=1, tiled=True)
    filt_re, filt_im, tables, kept_state = context
    back_grad = lax.optimization_barrier(
        causal_apply(grad_ch.astype(jnp.float32), filt_re, filt_im, tables, True).astype(
            jnp.bfloat16
        )
    )
    conv_ch, gate_ch = kept_state
    grad_wide = back_grad.astype(jnp.float32)
    conv_grad = lax.optimization_barrier((grad_wide * gate_ch).astype(jnp.bfloat16)).astype(
        jnp.float32
    )
    padded_grad = jnp.pad(conv_grad, ((0, 0), (0, tap_count - 1)))
    through = medium_backward(padded_grad, own_taps, conv_grad.shape[1])
    gate_grad = grad_wide * conv_ch * gate_ch * (1.0 - gate_ch)
    back_ch = (through + gate_grad).astype(jnp.bfloat16)
    returned = lax.all_to_all(back_ch, "seq", split_axis=1, concat_axis=0, tiled=True)
    partial_grad = jnp.dot(
        lax.all_gather(projection, "seq", axis=0, tiled=True),
        returned,
        preferred_element_type=jnp.float32,
    )
    input_grad = lax.psum_scatter(
        partial_grad.astype(jnp.bfloat16), "ch", scatter_dimension=0, tiled=True
    )
    return (conv_out, input_grad)


def solution(mesh):
    return jax.shard_map(
        on_device,
        mesh=mesh,
        in_specs=(
            P("ch", ("grp", "seq")),
            P("seq", "ch"),
            P("ch", None),
            P("ch", "seq"),
            P("ch", ("grp", "seq")),
        ),
        out_specs=(P("ch", ("grp", "seq")), P("ch", ("grp", "seq"))),
        check_vma=False,
    )
```

profile of v0, /device:TPU:0, one launch (start us, length us, event | category | flops | bytes accessed | tf_op | source)
XLA Modules:
  0.0 196.6 jit_solution(1277242276180059869)
XLA Ops:
  7.2 0.0 all-gather.5.cloned.1.call-start
  7.2 0.7 all-gather.5.cloned.1.call-update
  7.9 0.0 all-gather.3.cloned.1.call-start
  8.0 0.7 all-gather.3.cloned.1.call-update
  8.7 6.4 %all-to-all-start.3 = ((bf16[4,128,128]{2,1,0:T(8,128)(2,1)}), bf16[4,128,128]{2,1,0:T(8,128)(2,1)S(1)}, u32[]{:S(2)}, u32[]{:S(2)}) async-start(bf16[4,128,128]{2,1,0:T(8,128)(2,1)} %bitcast.137), calls=%async_computation.3 | async-start | bytes 262144 | tf_op jit(solution)/shard_map/all_to_all | solution.py:142
  15.0 3.3 %dynamic-slice_reduce_fusion.121 = (f32[128]{0:T(128)S(1)}, f32[128]{0:T(128)S(1)}, f32[128]{0:T(128)}, f32[128]{0:T(128)}, f32[128]{0:T(128)}, /*index=5*/f32[1...) fusion(f32[512,128]{1,0:T(8,128)} %param.7, ...), kind=kLoop, calls=%fused_computation.996 | loop fusion | bytes 17480 | tf_op jit(solution)/shard_map/slice | solution.py:17
  18.3 2.2 %dynamic-slice_reduce_fusion.120 = (f32[128]{0:T(128)}, f32[128]{0:T(128)}, f32[128]{0:T(128)}, f32[128]{0:T(128)}, f32[128]{0:T(128)}, /*index=5*/f32[128]{0:T(128)}, f32[128]{0:T(128)}, f32[128]{0:T(128)}) fusion(f32[512,128]{1,0:T(8,128)} %param.7, s32[]{:T(128)S(6)} %select_n.123, s32[]{:T(128)S(6)} %add.1346, s32[]{:T(128)S(6)} %add.1352, ...), kind=kLoop, calls=%fused_computation.995 | loop fusion | bytes 8228 | tf_op jit(solution)/shard_map/slice | solution.py:17
  20.5 1.3 dynamic-slice_reduce_fusion.122
  21.8 1.3 dynamic-slice_reduce_fusion.123
  23.1 1.3 dynamic-slice_reduce_fusion.124
  24.3 1.3 dynamic-slice_reduce_fusion.125
  25.6 1.3 dynamic-slice_reduce_fusion.126
  26.9 1.3 dynamic-slice_reduce_fusion.127
  28.2 0.1 fusion.649
  28.3 5.1 %all-to-all-start.1 = ((bf16[4,128,128]{2,1,0:T(8,128)(2,1)}), bf16[4,128,128]{2,1,0:T(8,128)(2,1)S(1)}, u32[]{:S(2)}, u32[]{:S(2)}) async-start(bf16[4,128,128]{2,1,0:T(8,128)(2,1)} %bitcast.11), calls=%async_computation.1 | async-start | bytes 262144 | tf_op jit(solution)/shard_map/all_to_all | solution.py:129
  33.3 0.4 convolution_negate_fusion
  33.7 0.4 fusion.573
  34.1 5.1 %all-to-all-done.1 = bf16[4,128,128]{2,1,0:T(8,128)(2,1)S(1)} async-done(((bf16[4,128,128]{2,1,0:T(8,128)(2,1)}), bf16[4,128,128]{2,1,0:T(8,128)(2,1)S(1)}, u32[]{:S(2)}, u32[]{:S(2)}) %all-to-all-start.1) | async-done | bytes 131104 | tf_op jit(solution)/shard_map/all_to_all | solution.py:129
  39.2 0.4 convolution_negate_fusion.1
  39.6 0.6 subtract_bitcast_fusion
  40.2 0.6 fusion.37
  40.8 0.6 fusion.39
  41.4 0.6 fusion.43
  42.1 0.6 convolution_subtract_fusion.3
  42.7 0.6 convolution_add_fusion.3
  43.3 0.6 convolution_add_fusion.1
  44.4 67.0 %all-gather.3.cloned.1.call-done = bf16[4096,512]{1,0:T(8,128)(2,1)} async-done(((bf16[1024,512]{1,0:T(8,128)(2,1)}), bf16[4096,512]{1,0:T(8,128)(2,1)}) %all-gather.3.cloned.1.call-update) | async-done | bytes 4194320 | tf_op jit(solution)/shard_map/all_gather | solution.py:117
  111.3 3.8 %convolution_convert_fusion.1 = bf16[512,128]{1,0:T(8,128)(2,1)S(1)} fusion(bf16[4096,512]{1,0:T(8,128)(2,1)} %all-gather.3.cloned.1.call-done, bf16[4096,128]{1,0:T(8,128)(2,1)} %all-gather.5.cloned.1.call-done), kind=kOutput, calls=%fused_computation.275 | convolution fusion | flops 536936448 | bytes 5373952 | tf_op jit(solution)/shard_map/dot_general | solution.py:116
  115.1 0.8 copy.57
  115.9 3.3 %all-to-all-start = ((bf16[4,128,128]{1,2,0:T(8,128)(2,1)}), bf16[4,128,128]{1,2,0:T(8,128)(2,1)S(1)}, u32[]{:S(2)}, u32[]{:S(2)}) async-start(bf16[4,128,128]{1,2,0:T(8,128)(2,1)} %copy.57), calls=%async_computation | async-start | bytes 262144 | tf_op jit(solution)/shard_map/all_to_all | solution.py:128
  119.2 0.0 reduce-scatter.2.cloned.1.call-start
  119.3 1.4 fusion.33
  120.7 4.6 %all-to-all-done = bf16[4,128,128]{1,2,0:T(8,128)(2,1)S(1)} async-done(((bf16[4,128,128]{1,2,0:T(8,128)(2,1)}), bf16[4,128,128]{1,2,0:T(8,128)(2,1)S(1)}, u32[]{:S(2)}, u32[]{:S(2)}) %all-to-all-start) | async-done | bytes 131104 | tf_op jit(solution)/shard_map/all_to_all | solution.py:128
  125.7 7.3 %multiply_convert_fusion = (bf16[128,512]{0,1:T(8,128)(2,1)S(1)}, f32[128,512]{0,1:T(8,128)S(1)}) fusion(bf16[4,128,128]{1,2,0:T(8,128)(2,1)S(1)} %all-to-all-done, f32[128]{0:T(128)S(1)} %copy-done.23, f32[128]{0:T(128)} %get-tuple-element.9, f32[128]{0:T(128)} %get-tuple-element.10, f32[128]{0:T(128)} %get-tuple-element.11, f32[128]{0:T(128)} %get-tuple-element.12, ...), kind=kLoop, calls=%fused_computation.856 | loop fusion | flops 17104896 | bytes 851968 | tf_op jit(solution)/shard_map/convert_element_type | solution.py:137
  133.0 0.1 copy.58
  133.2 0.4 fusion.1
  133.6 0.5 multiply_subtract_fusion.2
  134.1 0.6 fusion.45
  134.7 0.6 fusion.49
  135.4 0.6 convolution_subtract_fusion.4
  136.0 0.6 convolution_add_fusion.4
  136.6 1.8 multiply_add_fusion
  138.4 0.8 fusion.25
  139.2 0.8 fusion.21
  140.1 0.8 convolution_subtract_fusion
  140.9 0.8 convolution_add_fusion
  141.8 0.4 fusion.10
  142.2 0.4 fusion.5
  142.6 0.1 copy.83
  142.7 0.1 fusion.51
  142.8 7.5 %fusion.55 = bf16[128,512]{0,1:T(8,128)(2,1)S(1)} fusion(f32[128,512]{0,1:T(8,128)S(1)} %get-tuple-element.137, bf16[128,512]{0,1:T(8,128)(2,1)S(1)} %copy.83, f32[128,512]{0,1:T(8,128)S(1)} %convert_element_type.181, f32[128]{0:T(128)} %get-tuple-element.135, f32[128]{0:T(128)} %get-tuple-element.9, f32[128]{0:T(128)} %get-tuple-element.10, ...), kind=kLoop, calls=%fused_computation.339 | loop fusion | flops 17432576 | bytes 983040 | tf_op jit(solution)/shard_map/convert_element_type | solution.py:157
  150.3 0.1 copy.84
  150.4 8.6 %all_to_all.80 = bf16[128,4,128]{2,0,1:T(8,128)(2,1)S(1)} all-to-all(bf16[128,4,128]{2,0,1:T(8,128)(2,1)S(1)} %copy.84), channel_id=1, replica_groups=mesh['grp'=2,'seq'=4,'ch'=4] {'seq'}, dimensions={1} | all-to-all | bytes 262144 | tf_op jit(solution)/shard_map/all_to_all | solution.py:158
  159.0 4.7 %fusion = bf16[4096,128]{0,1:T(8,128)(2,1)} fusion(bf16[512,128]{1,0:T(8,128)(2,1)S(1)} %bitcast.136, bf16[4096,512]{1,0:T(8,128)(2,1)} %all-gather.3.cloned.1.call-done), kind=kOutput, calls=%fused_computation.1 | convolution fusion | flops 537395200 | bytes 5373952 | tf_op jit(solution)/shard_map/dot_general | solution.py:159
  163.7 0.8 fusion.27
  164.5 0.8 fusion.31
  165.4 0.8 convolution_add_fusion.2
  166.2 0.8 convolution_subtract_fusion.2
  167.0 0.4 fusion.17
  167.4 0.4 fusion.6
  167.9 8.4 %all_to_all.81 = bf16[128,4,128]{2,0,1:T(8,128)(2,1)S(1)} all-to-all(bf16[128,4,128]{2,0,1:T(8,128)(2,1)S(1)} %copy.73), channel_id=1, replica_groups=mesh['grp'=2,'seq'=4,'ch'=4] {'seq'}, dimensions={1} | all-to-all | bytes 262144 | tf_op jit(solution)/shard_map/all_to_all | solution.py:141
  176.3 11.3 %reduce-scatter.2.cloned.1.call-done = bf16[1024,128]{0,1:T(8,128)(2,1)} async-done(((bf16[4096,128]{0,1:T(8,128)(2,1)}), bf16[1024,128]{0,1:T(8,128)(2,1)}) %reduce-scatter.2.cloned.1.call-update) | async-done | bytes 262160 | tf_op jit(solution)/shard_map/reduce_scatter | solution.py:164
  187.6 1.8 copy.85
  189.4 0.7 copy.162
  (89 shorter events, 0.3 us)
Async XLA Ops:
  7.2 13.3 %copy-start = (f32[512,128]{1,0:T(8,128)S(1)}, f32[512,128]{1,0:T(8,128)}, u32[]{:S(2)}) copy-start(f32[512,128]{1,0:T(8,128)} %param.7) | copy-start | bytes 786436
  7.2 37.2 %all-gather.5.cloned.1.call-start = ((), (), s32[]{:S(2)}) async-start(), calls=%async_computation.7 | async-start | bytes 1310720 | tf_op jit(solution)/shard_map/all_gather | solution.py:115
  7.9 103.4 %all-gather.3.cloned.1.call-start = ((), (), s32[]{:S(2)}) async-start(), calls=%async_computation.6 | async-start | bytes 5242880 | tf_op jit(solution)/shard_map/all_gather | solution.py:117
  8.7 19.6 %all-to-all-start.3 = ((bf16[4,128,128]{2,1,0:T(8,128)(2,1)}), bf16[4,128,128]{2,1,0:T(8,128)(2,1)S(1)}, u32[]{:S(2)}, u32[]{:S(2)}) async-start(bf16[4,128,128]{2,1,0:T(8,128)(2,1)} %bitcast.137), calls=%async_computation.3 | async-start | bytes 262144 | tf_op jit(solution)/shard_map/all_to_all | solution.py:142
  28.3 11.0 %all-to-all-start.1 = ((bf16[4,128,128]{2,1,0:T(8,128)(2,1)}), bf16[4,128,128]{2,1,0:T(8,128)(2,1)S(1)}, u32[]{:S(2)}, u32[]{:S(2)}) async-start(bf16[4,128,128]{2,1,0:T(8,128)(2,1)} %bitcast.11), calls=%async_computation.1 | async-start | bytes 262144 | tf_op jit(solution)/shard_map/all_to_all | solution.py:129
  43.9 81.4 %copy-start.1 = (f32[128]{0:T(128)S(1)}, f32[128]{0:T(128)}, u32[]{:S(2)}) copy-start(f32[128]{0:T(128)} %get-tuple-element.113) | copy-start | bytes 1540
  43.9 81.4 %copy-start.2 = (f32[128]{0:T(128)S(1)}, f32[128]{0:T(128)}, u32[]{:S(2)}) copy-start(f32[128]{0:T(128)} %get-tuple-element.114) | copy-start | bytes 1540
  44.0 81.4 %copy-start.3 = (f32[128]{0:T(128)S(1)}, f32[128]{0:T(128)}, u32[]{:S(2)}) copy-start(f32[128]{0:T(128)} %get-tuple-element.115) | copy-start | bytes 1540
  44.0 81.4 %copy-start.4 = (f32[128]{0:T(128)S(1)}, f32[128]{0:T(128)}, u32[]{:S(2)}) copy-start(f32[128]{0:T(128)} %get-tuple-element.116) | copy-start | bytes 1540
  44.0 81.4 %copy-start.5 = (f32[128]{0:T(128)S(1)}, f32[128]{0:T(128)}, u32[]{:S(2)}) copy-start(f32[128]{0:T(128)} %get-tuple-element.117) | copy-start | bytes 1540
  44.0 81.4 %copy-start.6 = (f32[128]{0:T(128)S(1)}, f32[128]{0:T(128)}, u32[]{:S(2)}) copy-start(f32[128]{0:T(128)} %get-tuple-element.118) | copy-start | bytes 1540
  44.0 81.4 %copy-start.7 = (f32[128]{0:T(128)S(1)}, f32[128]{0:T(128)}, u32[]{:S(2)}) copy-start(f32[128]{0:T(128)} %get-tuple-element.119) | copy-start | bytes 1540
  44.0 81.4 %copy-start.8 = (f32[128]{0:T(128)S(1)}, f32[128]{0:T(128)}, u32[]{:S(2)}) copy-start(f32[128]{0:T(128)} %get-tuple-element.120) | copy-start | bytes 1540
  44.0 81.4 %copy-start.9 = (f32[128]{0:T(128)S(1)}, f32[128]{0:T(128)}, u32[]{:S(2)}) copy-start(f32[128]{0:T(128)} %get-tuple-element.121) | copy-start | bytes 1540
  44.0 81.4 %copy-start.10 = (f32[128]{0:T(128)S(1)}, f32[128]{0:T(128)}, u32[]{:S(2)}) copy-start(f32[128]{0:T(128)} %get-tuple-element.122) | copy-start | bytes 1540
  44.0 81.4 %copy-start.11 = (f32[128]{0:T(128)S(1)}, f32[128]{0:T(128)}, u32[]{:S(2)}) copy-start(f32[128]{0:T(128)} %get-tuple-element.123) | copy-start | bytes 1540
  44.0 81.4 %copy-start.12 = (f32[128]{0:T(128)S(1)}, f32[128]{0:T(128)}, u32[]{:S(2)}) copy-start(f32[128]{0:T(128)} %get-tuple-element.124) | copy-start | bytes 1540
  44.1 81.4 %copy-start.13 = (f32[128]{0:T(128)S(1)}, f32[128]{0:T(128)}, u32[]{:S(2)}) copy-start(f32[128]{0:T(128)} %get-tuple-element.125) | copy-start | bytes 1540
  44.1 81.4 %copy-start.14 = (f32[128]{0:T(128)S(1)}, f32[128]{0:T(128)}, u32[]{:S(2)}) copy-start(f32[128]{0:T(128)} %get-tuple-element.126) | copy-start | bytes 1540
  44.1 81.4 %copy-start.15 = (f32[128]{0:T(128)S(1)}, f32[128]{0:T(128)}, u32[]{:S(2)}) copy-start(f32[128]{0:T(128)} %get-tuple-element.127) | copy-start | bytes 1540
  44.1 81.4 %copy-start.16 = (f32[128]{0:T(128)S(1)}, f32[128]{0:T(128)}, u32[]{:S(2)}) copy-start(f32[128]{0:T(128)} %get-tuple-element.128) | copy-start | bytes 1540
  44.1 81.4 %copy-start.17 = (f32[128]{0:T(128)S(1)}, f32[128]{0:T(128)}, u32[]{:S(2)}) copy-start(f32[128]{0:T(128)} %get-tuple-element.129) | copy-start | bytes 1540
  44.1 81.4 %copy-start.18 = (f32[128]{0:T(128)S(1)}, f32[128]{0:T(128)}, u32[]{:S(2)}) copy-start(f32[128]{0:T(128)} %get-tuple-element.130) | copy-start | bytes 1540
  44.1 81.4 %copy-start.19 = (f32[128]{0:T(128)S(1)}, f32[128]{0:T(128)}, u32[]{:S(2)}) copy-start(f32[128]{0:T(128)} %get-tuple-element.131) | copy-start | bytes 1540
  44.1 81.4 %copy-start.20 = (f32[128]{0:T(128)S(1)}, f32[128]{0:T(128)}, u32[]{:S(2)}) copy-start(f32[128]{0:T(128)} %get-tuple-element.132) | copy-start | bytes 1540
  44.1 81.4 %copy-start.21 = (f32[128]{0:T(128)S(1)}, f32[128]{0:T(128)}, u32[]{:S(2)}) copy-start(f32[128]{0:T(128)} %get-tuple-element.133) | copy-start | bytes 1540
  44.2 81.4 %copy-start.22 = (f32[128]{0:T(128)S(1)}, f32[128]{0:T(128)}, u32[]{:S(2)}) copy-start(f32[128]{0:T(128)} %get-tuple-element.134) | copy-start | bytes 1540
  44.2 81.4 %copy-start.23 = (f32[128]{0:T(128)S(1)}, f32[128]{0:T(128)}, u32[]{:S(2)}) copy-start(f32[128]{0:T(128)} %get-tuple-element.135) | copy-start | bytes 1540
  44.2 81.4 %copy-start.24 = (f32[128]{0:T(128)S(1)}, f32[128]{0:T(128)}, u32[]{:S(2)}) copy-start(f32[128]{0:T(128)} %get-tuple-element.94) | copy-start | bytes 1540
  44.2 81.4 %copy-start.25 = (f32[128]{0:T(128)S(1)}, f32[128]{0:T(128)}, u32[]{:S(2)}) copy-start(f32[128]{0:T(128)} %get-tuple-element.95) | copy-start | bytes 1540
  44.2 81.4 %copy-start.26 = (f32[128]{0:T(128)S(1)}, f32[128]{0:T(128)}, u32[]{:S(2)}) copy-start(f32[128]{0:T(128)} %get-tuple-element.96) | copy-start | bytes 1540
  44.2 81.4 %copy-start.27 = (f32[128]{0:T(128)S(1)}, f32[128]{0:T(128)}, u32[]{:S(2)}) copy-start(f32[128]{0:T(128)} %get-tuple-element.97) | copy-start | bytes 1540
  44.2 81.4 %copy-start.28 = (f32[128]{0:T(128)S(1)}, f32[128]{0:T(128)}, u32[]{:S(2)}) copy-start(f32[128]{0:T(128)} %get-tuple-element.98) | copy-start | bytes 1540
  44.2 81.4 %copy-start.29 = (f32[128]{0:T(128)S(1)}, f32[128]{0:T(128)}, u32[]{:S(2)}) copy-start(f32[128]{0:T(128)} %get-tuple-element.99) | copy-start | bytes 1540
  44.2 81.4 %copy-start.30 = (f32[128]{0:T(128)S(1)}, f32[128]{0:T(128)}, u32[]{:S(2)}) copy-start(f32[128]{0:T(128)} %get-tuple-element.100) | copy-start | bytes 1540
  44.2 81.4 %copy-start.31 = (f32[128]{0:T(128)S(1)}, f32[128]{0:T(128)}, u32[]{:S(2)}) copy-start(f32[128]{0:T(128)} %get-tuple-element.101) | copy-start | bytes 1540
  44.3 81.4 %copy-start.32 = (f32[128]{0:T(128)S(1)}, f32[128]{0:T(128)}, u32[]{:S(2)}) copy-start(f32[128]{0:T(128)} %get-tuple-element.102) | copy-start | bytes 1540
  44.3 81.4 %copy-start.33 = (f32[128]{0:T(128)S(1)}, f32[128]{0:T(128)}, u32[]{:S(2)}) copy-start(f32[128]{0:T(128)} %get-tuple-element.103) | copy-start | bytes 1540
  44.3 81.4 %copy-start.34 = (f32[128]{0:T(128)S(1)}, f32[128]{0:T(128)}, u32[]{:S(2)}) copy-start(f32[128]{0:T(128)} %get-tuple-element.104) | copy-start | bytes 1540
  44.3 81.4 %copy-start.35 = (f32[128]{0:T(128)S(1)}, f32[128]{0:T(128)}, u32[]{:S(2)}) copy-start(f32[128]{0:T(128)} %get-tuple-element.105) | copy-start | bytes 1540
  44.3 81.4 %copy-start.36 = (f32[128]{0:T(128)S(1)}, f32[128]{0:T(128)}, u32[]{:S(2)}) copy-start(f32[128]{0:T(128)} %get-tuple-element.106) | copy-start | bytes 1540
  44.3 81.4 %copy-start.37 = (f32[128]{0:T(128)S(1)}, f32[128]{0:T(128)}, u32[]{:S(2)}) copy-start(f32[128]{0:T(128)} %get-tuple-element.107) | copy-start | bytes 1540
  44.3 81.4 %copy-start.38 = (f32[128]{0:T(128)S(1)}, f32[128]{0:T(128)}, u32[]{:S(2)}) copy-start(f32[128]{0:T(128)} %get-tuple-element.108) | copy-start | bytes 1540
  44.3 81.4 %copy-start.39 = (f32[128]{0:T(128)S(1)}, f32[128]{0:T(128)}, u32[]{:S(2)}) copy-start(f32[128]{0:T(128)} %get-tuple-element.109) | copy-start | bytes 1540
  44.3 81.4 %copy-start.40 = (f32[128]{0:T(128)S(1)}, f32[128]{0:T(128)}, u32[]{:S(2)}) copy-start(f32[128]{0:T(128)} %get-tuple-element.110) | copy-start | bytes 1540
  115.9 9.4 %all-to-all-start = ((bf16[4,128,128]{1,2,0:T(8,128)(2,1)}), bf16[4,128,128]{1,2,0:T(8,128)(2,1)S(1)}, u32[]{:S(2)}, u32[]{:S(2)}) async-start(bf16[4,128,128]{1,2,0:T(8,128)(2,1)} %copy.57), calls=%async_computation | async-start | bytes 262144 | tf_op jit(solution)/shard_map/all_to_all | solution.py:128
  119.2 68.4 %reduce-scatter.2.cloned.1.call-start = ((), (), s32[]{:S(2)}) async-start(), calls=%async_computation.8 | async-start | bytes 1310720 | tf_op jit(solution)/shard_map/reduce_scatter | solution.py:164
Sparse Core Ops, SparseCore 0:
  9.5 19.4 all-gather.4
  30.6 80.7 all-gather.2
  163.8 23.7 reduce-scatter.1
where the time goes:
time: 197 us
  waiting for transfers between devices  89.4 us (45%)
  matrix products  28.7 us (15%)
  local copies, waits for them, and re-layouts  17 us (9%)
  blocking collectives  17 us (9%)
  other arithmetic  15 us (8%)
  starting transfers between devices  14.9 us (8%)
  between operations  14.7 us (7%)
    all_gather x1, waiting for transfers between devices, on_device(): lax.all_gather(projection, 'seq', axis=0, tiled=True)  67 us
    slice x8, local copies, waits for them, and re-layouts, medium_forward(): tap_weights[:, offset:offset + 1] * padded[:, begin_col:begin_col + length]  13.2 us
    reduce_scatter x1, waiting for transfers between devices, on_device(): lax.psum_scatter(partial_grad.astype(jnp.bfloat16), 'ch', scatter_dimensi...  11.3 us
    all_to_all x1, blocking collectives, on_device(): lax.all_to_all(back_ch, 'seq', split_axis=1, concat_axis=0, tiled=True)  8.57 us
    all_to_all x1, blocking collectives, on_device(): lax.all_to_all(output_ch, 'seq', split_axis=1, concat_axis=0, tiled=True)  8.41 us
    convert_element_type x1, other arithmetic, on_device(): back_ch = (through + gate_grad).astype(jnp.bfloat16)  7.47 us
    convert_element_type x1, other arithmetic, on_device(): (conv_ch * gate_ch).astype(jnp.bfloat16)  7.34 us
    all_to_all x1, starting transfers between devices, on_device(): lax.all_to_all(cotangent, 'seq', split_axis=0, concat_axis=1, tiled=True)  6.36 us
  transfers between devices with their start and end apart: 6, of which 4 were waited for; matrix products, arithmetic and copies ran while one was open for 12% of the time, Pallas kernels for 0%

commit v1 on v0

--- a/solution.py
+++ b/solution.py
@@ -1,8 +1,12 @@
+import functools
 import math
 
 import jax
 import jax.numpy as jnp
+import numpy as np
 from jax import lax
+from jax.experimental import pallas as pl
+from jax.experimental.pallas import tpu as pltpu
 from jax.sharding import PartitionSpec as P
 
 exact_mode = lax.Precision.HIGH
@@ -167,9 +171,358 @@
     return (conv_out, input_grad)
 
 
+MESH = pl.DeviceIdType.MESH
+
+
+def transform_table(length):
+    points = 2 * length
+    turns = np.arange(length)[:, None] * (2 * np.arange(length)[None, :] + 1) % (2 * points)
+    angles = turns * (math.pi / points)
+    return jnp.asarray(np.concatenate([np.cos(angles), np.sin(angles)], axis=1), jnp.bfloat16)
+
+
+def to_spectrum(signal, table):
+    spectrum = jnp.dot(signal, table, preferred_element_type=jnp.float32)
+    half = spectrum.shape[1] // 2
+    return spectrum[:, :half], spectrum[:, half:]
+
+
+def from_spectrum(even, odd, table):
+    both = jnp.concatenate([even, odd], axis=1).astype(jnp.bfloat16)
+    signal = lax.dot_general(
+        both, table, (((1,), (1,)), ((), ())), preferred_element_type=jnp.float32
+    )
+    return signal * (1.0 / table.shape[0])
+
+
+def times(left, right):
+    return left[0] * right[0] - left[1] * right[1], left[0] * right[1] + left[1] * right[0]
+
+
+def times_conj(left, right):
+    return left[0] * right[0] + left[1] * right[1], left[1] * right[0] - left[0] * right[1]
+
+
+def stacked(first, second):
+    return (
+        jnp.concatenate([first[0], second[0]], axis=0),
+        jnp.concatenate([first[1], second[1]], axis=0),
+    )
+
+
+def fused_kernel(
+    ns,
+    nc,
+    pieces,
+    act_ref,
+    proj_ref,
+    taps_ref,
+    filt_ref,
+    cot_ref,
+    table_ref,
+    conv_ref,
+    grad_ref,
+    held_act,
+    all_act,
+    wide_in,
+    part_sum,
+    got_sum,
+    conv_own,
+    conv_got,
+    all_grad,
+    part_grad,
+    pair_grad,
+    mirror_send,
+    mirror_got,
+    total_grad,
+    turned,
+    grad_got,
+    send_sems,
+    recv_sems,
+):
+    s = lax.axis_index("seq")
+    h = lax.axis_index("ch")
+    rows = act_ref.shape[0]
+    span = act_ref.shape[1]
+    own = filt_ref.shape[0] // ns
+    quarter = rows // nc
+    piece = quarter // pieces
+    length = span * ns
+    partner = h + 1 - 2 * (h % 2)
+    mirror = (h + nc // 2) % nc
+    across = (partner + nc // 2) % nc
+    started = []
+
+    def block(index, size):
+        return pl.ds(pl.multiple_of(index * size, size), size)
+
+    def part(index, k):
+        return pl.ds(pl.multiple_of(index * quarter + k * piece, piece), piece)
+
+    def send(src, dst, **where):
+        slot = len(started)
+        copy = pltpu.make_async_remote_copy(
+            src_ref=src,
+            dst_ref=dst,
+            send_sem=send_sems.at[slot],
+            recv_sem=recv_sems.at[slot],
+            device_id=where,
+            device_id_type=MESH,
+        )
+        copy.start()
+        started.append(copy)
+        return copy
+
+    barrier = pltpu.get_barrier_semaphore()
+    for d in range(1, ns):
+        pl.semaphore_signal(
+            barrier, inc=1, device_id={"seq": (s + d) % ns}, device_id_type=MESH
+        )
+    for d in range(1, nc):
+        pl.semaphore_signal(barrier, inc=1, device_id={"ch": (h + d) % nc}, device_id_type=MESH)
+    pl.semaphore_wait(barrier, ns + nc - 2)
+
+    spread = []
+    for k in range(pieces):
+        spread.append(
+            [
+                send(
+                    act_ref.at[part((h + d) % nc, k), :],
+                    held_act.at[h, pl.ds(k * piece, piece), :],
+                    ch=(h + d) % nc,
+                )
+                for d in range(1, nc)
+            ]
+        )
+    held_act[h] = act_ref[block(h, quarter), :]
+    moved = []
+    for k in range(pieces):
+        for copy in spread[k]:
+            copy.wait_recv()
+        moved.append(
+            [
+                send(
+                    held_act.at[(s + d) % ns, pl.ds(k * piece, piece), :],
+                    all_act.at[part(h, k), block(s, span)],
+                    seq=(s + d) % ns,
+                )
+                for d in range(1, ns)
+            ]
+        )
+    all_act[block(h, quarter), block(s, span)] = held_act[s]
+    wide = []
+    for at, ref in enumerate((filt_ref, cot_ref)):
+        for d in range(1, ns):
+            wide.append(
+                send(
+                    ref.at[block((s + d) % ns, own), :],
+                    wide_in.at[pl.ds(at * own, own), block(s, span)],
+                    seq=(s + d) % ns,
+                )
+            )
+        wide_in[pl.ds(at * own, own), block(s, span)] = ref[block(s, own), :]
+    shared, crossed = [], []
+    for k in range(pieces):
+        for copy in moved[k]:
+            copy.wait_recv()
+        crossed.append(send(all_act.at[part(h, k), :], all_act.at[part(h, k), :], ch=mirror))
+        shared.append(send(all_act.at[part(h, k), :], all_act.at[part(h, k), :], ch=partner))
+
+    for copy in wide:
+        copy.wait_recv()
+    table = table_ref[...]
+    spec = to_spectrum(wide_in[...], table)
+    filt = (spec[0][:own], spec[1][:own])
+    cot = (spec[0][own:], spec[1][own:])
+    taps_own = taps_ref[block(s, own), :]
+    taps_high = taps_own.astype(jnp.bfloat16)
+    taps_low = (taps_own - taps_high.astype(jnp.float32)).astype(jnp.bfloat16)
+    table_top = table_ref[pl.ds(0, taps_own.shape[1]), :]
+    high = to_spectrum(taps_high, table_top)
+    low = to_spectrum(taps_low, table_top)
+    taps = (high[0] + low[0], high[1] + low[1])
+    back = from_spectrum(*times_conj(cot, filt), table).astype(jnp.bfloat16).astype(jnp.float32)
+
+    for k in range(pieces):
+        crossed[k].wait_recv()
+        shared.append(
+            send(all_act.at[part(mirror, k), :], all_act.at[part(mirror, k), :], ch=partner)
+        )
+    for copy in shared:
+        copy.wait_recv()
+
+    summed = lax.dot_general(
+        proj_ref[...],
+        all_act[...],
+        (((0,), (0,)), ((), ())),
+        preferred_element_type=jnp.float32,
+    )
+    part_sum[...] = summed.astype(jnp.bfloat16)
+    reduced = [
+        send(
+            part_sum.at[block((s + d) % ns, own), :],
+            got_sum.at[d - 1],
+            seq=(s + d) % ns,
+        )
+        for d in range(1, ns)
+    ]
+    mixed = part_sum[block(s, own), :].astype(jnp.float32)
+    for d in range(1, ns):
+        reduced[d - 1].wait_recv()
+        mixed = mixed + got_sum[d - 1].astype(jnp.float32)
+    values = mixed.astype(jnp.bfloat16)
+    gate = jax.nn.sigmoid(values.astype(jnp.float32))
+    grad_medium = (back * gate).astype(jnp.bfloat16)
+    spec = to_spectrum(jnp.concatenate([values, grad_medium], axis=0), table)
+    both = stacked(
+        times((spec[0][:own], spec[1][:own]), taps),
+        times_conj((spec[0][own:], spec[1][own:]), taps),
+    )
+    both = from_spectrum(*both, table)
+    medium, through = both[:own], both[own:]
+    all_grad[block(s, own), :] = (through + back * medium * gate * (1.0 - gate)).astype(
+        jnp.bfloat16
+    )
+    gathered = [
+        send(all_grad.at[block(s, own), :], all_grad.at[block(s, own), :], seq=(s + d) % ns)
+        for d in range(1, ns)
+    ]
+
+    gated = (medium * gate).astype(jnp.bfloat16)
+    conv = from_spectrum(*times(to_spectrum(gated, table), filt), table)
+    conv_own[...] = conv.astype(jnp.bfloat16)
+    returned = [
+        send(
+            conv_own.at[:, block((s + d) % ns, span)],
+            conv_got.at[block(s, own), :],
+            seq=(s + d) % ns,
+        )
+        for d in range(1, ns)
+    ]
+    conv_got[block(s, own), :] = conv_own[:, block(s, span)]
+
+    for copy in gathered:
+        copy.wait_recv()
+    first, second = [], []
+    for k in range(pieces):
+        for to, copies in ((across, first), (partner, second)):
+            got = jnp.dot(
+                proj_ref[part(to, k), :], all_grad[...], preferred_element_type=jnp.float32
+            )
+            part_grad[part(to, k), :] = got.astype(jnp.bfloat16)
+            side = 0 if copies is first else 1
+            copies.append(
+                send(
+                    part_grad.at[part(to, k), :],
+                    pair_grad.at[side, pl.ds(k * piece, piece), :],
+                    ch=partner,
+                )
+            )
+    mirrored = []
+    for k in range(pieces):
+        at = pl.ds(k * piece, piece)
+        kept = jnp.dot(
+            proj_ref[part(mirror, k), :], all_grad[...], preferred_element_type=jnp.float32
+        )
+        first[k].wait_recv()
+        kept = kept + pair_grad[0, at, :].astype(jnp.float32)
+        mirror_send[at, :] = kept.astype(jnp.bfloat16)
+        mirrored.append(send(mirror_send.at[at, :], mirror_got.at[at, :], ch=mirror))
+    placed = []
+    for k in range(pieces):
+        at = pl.ds(k * piece, piece)
+        kept = jnp.dot(proj_ref[part(h, k), :], all_grad[...], preferred_element_type=jnp.float32)
+        second[k].wait_recv()
+        kept = kept + pair_grad[1, at, :].astype(jnp.float32)
+        mirrored[k].wait_recv()
+        kept = kept + mirror_got[at, :].astype(jnp.float32)
+        total_grad[at, :] = kept.astype(jnp.bfloat16)
+        placed.append(
+            [
+                send(
+                    total_grad.at[at, block((s + d) % ns, span)],
+                    turned.at[s, at, :],
+                    seq=(s + d) % ns,
+                )
+                for d in range(1, ns)
+            ]
+        )
+        turned[s, at, :] = total_grad[at, block(s, span)]
+    final = []
+    for k in range(pieces):
+        at = pl.ds(k * piece, piece)
+        for copy in placed[k]:
+            copy.wait_recv()
+        final += [
+            send(turned.at[(h + d) % nc, at, :], grad_got.at[part(h, k), :], ch=(h + d) % nc)
+            for d in range(1, nc)
+        ]
+        grad_got[part(h, k), :] = turned[h, at, :]
+    for copy in returned:
+        copy.wait_recv()
+    conv_ref[...] = conv_got[...]
+    for copy in final:
+        copy.wait_recv()
+    grad_ref[...] = grad_got[...]
+    for copy in started:
+        copy.wait_send()
+
+
+def fused_on_device(ns, nc, activations, projection, medium_taps, long_filters, cotangent):
+    rows, span = activations.shape
+    channels = long_filters.shape[0]
+    own = channels // ns
+    length = span * ns
+    quarter = rows // nc
+    pieces = 2
+    copies = 9 * pieces + 3 * pieces + 3 * pieces + 6 * pieces + 24 + 16
+    vmem = pl.BlockSpec(memory_space=pltpu.VMEM)
+    bf16 = jnp.bfloat16
+    return pl.pallas_call(
+        functools.partial(fused_kernel, ns, nc, pieces),
+        out_shape=(
+            jax.ShapeDtypeStruct((channels, span), bf16),
+            jax.ShapeDtypeStruct((rows, span), bf16),
+        ),
+        in_specs=[vmem] * 6,
+        out_specs=(vmem, vmem),
+        scratch_shapes=[
+            pltpu.VMEM((nc, quarter, span), bf16),
+            pltpu.VMEM((rows, length), bf16),
+            pltpu.VMEM((2 * own, length), bf16),
+            pltpu.VMEM((channels, length), bf16),
+            pltpu.VMEM((ns - 1, own, length), bf16),
+            pltpu.VMEM((own, length), bf16),
+            pltpu.VMEM((channels, span), bf16),
+            pltpu.VMEM((channels, length), bf16),
+            pltpu.VMEM((rows, length), bf16),
+            pltpu.VMEM((2, quarter, length), bf16),
+            pltpu.VMEM((quarter, length), bf16),
+            pltpu.VMEM((quarter, length), bf16),
+            pltpu.VMEM((quarter, length), bf16),
+            pltpu.VMEM((ns, quarter, span), bf16),
+            pltpu.VMEM((rows, span), bf16),
+            pltpu.SemaphoreType.DMA((copies,)),
+            pltpu.SemaphoreType.DMA((copies,)),
+        ],
+        compiler_params=pltpu.CompilerParams(
+            collective_id=0, has_side_effects=True, vmem_limit_bytes=48 * 1024 * 1024
+        ),
+    )(activations, projection, medium_taps, long_filters, cotangent, transform_table(length))
+
+
 def solution(mesh):
+    ns, nc = mesh.shape["seq"], mesh.shape["ch"]
+
+    def on_any(activations, projection, medium_taps, long_filters, cotangent):
+        arrays = (activations, projection, medium_taps, long_filters, cotangent)
+        table_bytes = 4 * (activations.shape[1] * ns) ** 2
+        if ns == nc == 4 and table_bytes <= 4 << 20:
+            return fused_on_device(ns, nc, *arrays)
+        return on_device(*arrays)
+
     return jax.shard_map(
-        on_device,
+        on_any,
         mesh=mesh,
         in_specs=(
             P("ch", ("grp", "seq")),

time: 197 us -> 79.2 us (0.40)
  waiting for transfers between devices: 89.4 us -> 0 us
  Pallas kernels: 0 us -> 70.7 us
  matrix products: 28.7 us -> 0 us
  blocking collectives: 17 us -> 0 us
  other arithmetic: 15 us -> 0 us
  starting transfers between devices: 14.9 us -> 0 us
  between operations: 14.7 us -> 0.65 us
  local copies, waits for them, and re-layouts: 17 us -> 7.51 us
    pallas_call x0 -> x1, Pallas kernels: none -> 70.7 us  [fused_on_device(): pl.pallas_call(functools.partial(fused_kernel, ns, nc, pieces), out_shape...]
    all_gather x2 -> x0, waiting for transfers between devices: 67 us -> none  [the longest x1 67 us: on_device(): lax.all_gather(projection, 'seq', axis=0, tiled=True)]
    dot_general x32 -> x0, matrix products: 28.7 us -> none  [the longest x1 4.65 us: on_device(): jnp.dot(lax.all_gather(projection, 'seq', axis=0, tiled=True), returned,...]
    all_to_all x2 -> x0, blocking collectives: 17 us -> none  [the longest x1 8.57 us: on_device(): lax.all_to_all(back_ch, 'seq', split_axis=1, concat_axis=0, tiled=True)]
    convert_element_type x5 -> x0, other arithmetic: 14.9 us -> none  [the longest x1 7.47 us: on_device(): back_ch = (through + gate_grad).astype(jnp.bfloat16)]
    all_to_all x3 -> x0, starting transfers between devices: 14.7 us -> none  [the longest x1 6.36 us: on_device(): lax.all_to_all(cotangent, 'seq', split_axis=0, concat_axis=1, tiled=True)]
    slice x8 -> x0, local copies, waits for them, and re-layouts: 13.2 us -> none  [medium_forward(): tap_weights[:, offset:offset + 1] * padded[:, begin_col:begin_col + length]]
    reduce_scatter x1 -> x0, waiting for transfers between devices: 11.3 us -> none  [on_device(): lax.psum_scatter(partial_grad.astype(jnp.bfloat16), 'ch', scatter_dimensi...]
  transfers between devices with their start and end apart: 6 -> 0, of which waited for: 4 -> 0; matrix products, arithmetic and copies ran while one was open for 12% -> 0% of each run, Pallas kernels for 0% -> 0%
where the time goes in v1:
time: 79.2 us; the launch traced here: 78.9 us
  Pallas kernels  70.7 us (89%)
  local copies, waits for them, and re-layouts  7.51 us (9%)
    pallas_call x1, Pallas kernels, fused_on_device(): pl.pallas_call(functools.partial(fused_kernel, ns, nc, pieces), out_shape...  70.7 us
    unnamed x14, local copies, waits for them, and re-layouts  7.51 us

profile of v1, /device:TPU:0, one launch (start us, length us, event | category | flops | bytes accessed | tf_op | source)
XLA Modules:
  0.0 78.9 jit_solution(8140230834550911341)
XLA Ops:
  0.6 0.0 copy-start
  0.6 1.2 %copy-done = bf16[1024,512]{1,0:T(8,128)(2,1)S(1)} copy-done((bf16[1024,512]{1,0:T(8,128)(2,1)S(1)}, bf16[1024,512]{1,0:T(8,128)(2,1)}, u32[]{:S(2)}) %copy-start) | copy-done | bytes 1048600
  1.9 0.0 copy-start.1
  1.9 1.2 %copy-done.1 = bf16[512,1024]{1,0:T(8,128)(2,1)S(1)} copy-done((bf16[512,1024]{1,0:T(8,128)(2,1)S(1)}, bf16[512,1024]{1,0:T(8,128)(2,1)}, u32[]{:S(2)}) %copy-start.1) | copy-done | bytes 1048600
  3.1 0.0 copy-start.2
  3.1 0.9 %copy-done.2 = bf16[1024,128]{1,0:T(8,128)(2,1)S(1)} copy-done((bf16[1024,128]{1,0:T(8,128)(2,1)S(1)}, bf16[1024,128]{1,0:T(8,128)(2,1)}, u32[]{:S(2)}) %copy-start.2) | copy-done | bytes 262168
  4.0 0.0 copy-start.3
  4.0 0.9 %copy-done.3 = f32[512,128]{1,0:T(8,128)S(1)} copy-done((f32[512,128]{1,0:T(8,128)S(1)}, f32[512,128]{1,0:T(8,128)}, u32[]{:S(2)}) %copy-start.3) | copy-done | bytes 262168
  5.0 0.0 copy-start.4
  5.0 0.9 %copy-done.4 = bf16[512,128]{1,0:T(8,128)(2,1)S(1)} copy-done((bf16[512,128]{1,0:T(8,128)(2,1)S(1)}, bf16[512,128]{1,0:T(8,128)(2,1)}, u32[]{:S(2)}) %copy-start.4) | copy-done | bytes 131096
  5.9 0.0 copy-start.5
  5.9 0.9 %copy-done.5 = bf16[512,128]{1,0:T(8,128)(2,1)S(1)} copy-done((bf16[512,128]{1,0:T(8,128)(2,1)S(1)}, bf16[512,128]{1,0:T(8,128)(2,1)}, u32[]{:S(2)}) %copy-start.5) | copy-done | bytes 131096
  6.8 70.7 %shard_map.77 = (bf16[512,128]{1,0:T(8,128)(2,1)S(1)}, bf16[1024,128]{1,0:T(8,128)(2,1)S(1)}) custom-call(bf16[1024,128]{1,0:T(8,128)(2,1)S(1)} %copy-done.2, bf16[1024,512]{1,0:T(8,128)(2,1)S(1)} %copy-done, f32[512,128]{1,0:T(8,128)S(1)} %copy-done.3, bf16[512,128]{1,0:T(8,128)(2,1)S(1)} %copy-done.4, bf16[512,128]{1,0:T(8,128)(2,1)S(1)} %copy-done.5, ...), custom_call_target="tpu_custom_call" | custom-call | tf_op jit(solution)/shard_map/pallas_call | solution.py:481
  77.5 0.7 copy.10
  78.2 0.7 copy.11
Async XLA Ops:
  0.6 1.2 %copy-start = (bf16[1024,512]{1,0:T(8,128)(2,1)S(1)}, bf16[1024,512]{1,0:T(8,128)(2,1)}, u32[]{:S(2)}) copy-start(bf16[1024,512]{1,0:T(8,128)(2,1)} %proj_ref.1) | copy-start | bytes 3145732
  1.9 1.2 %copy-start.1 = (bf16[512,1024]{1,0:T(8,128)(2,1)S(1)}, bf16[512,1024]{1,0:T(8,128)(2,1)}, u32[]{:S(2)}) copy-start(bf16[512,1024]{1,0:T(8,128)(2,1)} %constant.2.clone.table_ref) | copy-start | bytes 3145732
  3.1 0.9 %copy-start.2 = (bf16[1024,128]{1,0:T(8,128)(2,1)S(1)}, bf16[1024,128]{1,0:T(8,128)(2,1)}, u32[]{:S(2)}) copy-start(bf16[1024,128]{1,0:T(8,128)(2,1)} %act_ref.1) | copy-start | bytes 786436
  4.0 0.9 %copy-start.3 = (f32[512,128]{1,0:T(8,128)S(1)}, f32[512,128]{1,0:T(8,128)}, u32[]{:S(2)}) copy-start(f32[512,128]{1,0:T(8,128)} %taps_ref.1) | copy-start | bytes 786436
  5.0 0.9 %copy-start.4 = (bf16[512,128]{1,0:T(8,128)(2,1)S(1)}, bf16[512,128]{1,0:T(8,128)(2,1)}, u32[]{:S(2)}) copy-start(bf16[512,128]{1,0:T(8,128)(2,1)} %filt_ref.1) | copy-start | bytes 393220
  5.9 0.9 %copy-start.5 = (bf16[512,128]{1,0:T(8,128)(2,1)S(1)}, bf16[512,128]{1,0:T(8,128)(2,1)}, u32[]{:S(2)}) copy-start(bf16[512,128]{1,0:T(8,128)(2,1)} %cot_ref.1) | copy-start | bytes 393220

commit v2 on v1

--- a/solution.py
+++ b/solution.py
@@ -237,8 +237,13 @@
     total_grad,
     turned,
     grad_got,
+    proj_v,
+    proj_t,
+    taps_v,
+    table_v,
     send_sems,
     recv_sems,
+    load_sems,
 ):
     s = lax.axis_index("seq")
     h = lax.axis_index("ch")
@@ -251,7 +256,8 @@
     partner = h + 1 - 2 * (h % 2)
     mirror = (h + nc // 2) % nc
     across = (partner + nc // 2) % nc
-    started = []
+    started, loads = [], []
+    half = own // 2
 
     def block(index, size):
         return pl.ds(pl.multiple_of(index * size, size), size)
@@ -273,6 +279,12 @@
         started.append(copy)
         return copy
 
+    def load(src, dst):
+        copy = pltpu.make_async_copy(src, dst, load_sems.at[len(loads)])
+        copy.start()
+        loads.append(copy)
+        return copy
+
     barrier = pltpu.get_barrier_semaphore()
     for d in range(1, ns):
         pl.semaphore_signal(
@@ -280,6 +292,16 @@
         )
     for d in range(1, nc):
         pl.semaphore_signal(barrier, inc=1, device_id={"ch": (h + d) % nc}, device_id_type=MESH)
+    act_own = load(act_ref.at[block(h, quarter), :], held_act.at[h])
+    wide_own = [
+        load(ref.at[block(s, own), :], wide_in.at[pl.ds(at * own, own), block(s, span)])
+        for at, ref in enumerate((filt_ref, cot_ref))
+    ]
+    rest = [
+        load(table_ref, table_v),
+        load(taps_ref.at[block(s, own), :], taps_v),
+        load(proj_ref, proj_v),
+    ]
     pl.semaphore_wait(barrier, ns + nc - 2)
 
     spread = []
@@ -294,7 +316,7 @@
                 for d in range(1, nc)
             ]
         )
-    held_act[h] = act_ref[block(h, quarter), :]
+    act_own.wait()
     moved = []
     for k in range(pieces):
         for copy in spread[k]:
@@ -320,7 +342,6 @@
                     seq=(s + d) % ns,
                 )
             )
-        wide_in[pl.ds(at * own, own), block(s, span)] = ref[block(s, own), :]
     shared, crossed = [], []
     for k in range(pieces):
         for copy in moved[k]:
@@ -328,16 +349,22 @@
         crossed.append(send(all_act.at[part(h, k), :], all_act.at[part(h, k), :], ch=mirror))
         shared.append(send(all_act.at[part(h, k), :], all_act.at[part(h, k), :], ch=partner))
 
+    for copy in rest:
+        copy.wait()
+    for at in range(ns):
+        proj_t[pl.ds(at * own, own), :] = proj_v[:, pl.ds(at * own, own)].T
+    for copy in wide_own:
+        copy.wait()
     for copy in wide:
         copy.wait_recv()
-    table = table_ref[...]
+    table = table_v[...]
     spec = to_spectrum(wide_in[...], table)
     filt = (spec[0][:own], spec[1][:own])
     cot = (spec[0][own:], spec[1][own:])
-    taps_own = taps_ref[block(s, own), :]
+    taps_own = taps_v[...]
     taps_high = taps_own.astype(jnp.bfloat16)
     taps_low = (taps_own - taps_high.astype(jnp.float32)).astype(jnp.bfloat16)
-    table_top = table_ref[pl.ds(0, taps_own.shape[1]), :]
+    table_top = table_v[pl.ds(0, taps_own.shape[1]), :]
     high = to_spectrum(taps_high, table_top)
     low = to_spectrum(taps_low, table_top)
     taps = (high[0] + low[0], high[1] + low[1])
@@ -351,42 +378,58 @@
     for copy in shared:
         copy.wait_recv()
 
-    summed = lax.dot_general(
-        proj_ref[...],
-        all_act[...],
-        (((0,), (0,)), ((), ())),
-        preferred_element_type=jnp.float32,
-    )
-    part_sum[...] = summed.astype(jnp.bfloat16)
-    reduced = [
-        send(
-            part_sum.at[block((s + d) % ns, own), :],
-            got_sum.at[d - 1],
+    def half_of(index, c):
+        return pl.ds(pl.multiple_of(index * own + c * half, half), half)
+
+    def sum_to(d, c):
+        return send(
+            part_sum.at[half_of((s + d) % ns, c), :],
+            got_sum.at[d - 1, pl.ds(c * half, half), :],
             seq=(s + d) % ns,
         )
-        for d in range(1, ns)
-    ]
-    mixed = part_sum[block(s, own), :].astype(jnp.float32)
+
+    reduced = [[], []]
     for d in range(1, ns):
-        reduced[d - 1].wait_recv()
-        mixed = mixed + got_sum[d - 1].astype(jnp.float32)
-    values = mixed.astype(jnp.bfloat16)
-    gate = jax.nn.sigmoid(values.astype(jnp.float32))
-    grad_medium = (back * gate).astype(jnp.bfloat16)
-    spec = to_spectrum(jnp.concatenate([values, grad_medium], axis=0), table)
-    both = stacked(
-        times((spec[0][:own], spec[1][:own]), taps),
-        times_conj((spec[0][own:], spec[1][own:]), taps),
-    )
-    both = from_spectrum(*both, table)
-    medium, through = both[:own], both[own:]
-    all_grad[block(s, own), :] = (through + back * medium * gate * (1.0 - gate)).astype(
-        jnp.bfloat16
-    )
-    gathered = [
-        send(all_grad.at[block(s, own), :], all_grad.at[block(s, own), :], seq=(s + d) % ns)
-        for d in range(1, ns)
-    ]
+        got = jnp.dot(
+            proj_t[block((s + d) % ns, own), :],
+            all_act[...],
+            preferred_element_type=jnp.float32,
+        )
+        part_sum[block((s + d) % ns, own), :] = got.astype(jnp.bfloat16)
+        reduced[0].append(sum_to(d, 0))
+    for d in range(1, ns):
+        reduced[1].append(sum_to(d, 1))
+    mixed = jnp.dot(
+        proj_t[block(s, own), :], all_act[...], preferred_element_type=jnp.float32
+    )
+    gathered, mediums, gates = [], [], []
+    for c in range(2):
+        at = slice(c * half, (c + 1) * half)
+        summed = mixed[at]
+        for d in range(1, ns):
+            reduced[c][d - 1].wait_recv()
+            summed = summed + got_sum[d - 1, pl.ds(c * half, half), :].astype(jnp.float32)
+        values = summed.astype(jnp.bfloat16)
+        gate = jax.nn.sigmoid(values.astype(jnp.float32))
+        grad_medium = (back[at] * gate).astype(jnp.bfloat16)
+        spec = to_spectrum(jnp.concatenate([values, grad_medium], axis=0), table)
+        taps_half = (taps[0][at], taps[1][at])
+        both = stacked(
+            times((spec[0][:half], spec[1][:half]), taps_half),
+            times_conj((spec[0][half:], spec[1][half:]), taps_half),
+        )
+        both = from_spectrum(*both, table)
+        medium, through = both[:half], both[half:]
+        all_grad[half_of(s, c), :] = (
+            through + back[at] * medium * gate * (1.0 - gate)
+        ).astype(jnp.bfloat16)
+        gathered += [
+            send(all_grad.at[half_of(s, c), :], all_grad.at[half_of(s, c), :], seq=(s + d) % ns)
+            for d in range(1, ns)
+        ]
+        mediums.append(medium)
+        gates.append(gate)
+    medium, gate = jnp.concatenate(mediums, axis=0), jnp.concatenate(gates, axis=0)
 
     gated = (medium * gate).astype(jnp.bfloat16)
     conv = from_spectrum(*times(to_spectrum(gated, table), filt), table)
@@ -407,7 +450,7 @@
     for k in range(pieces):
         for to, copies in ((across, first), (partner, second)):
             got = jnp.dot(
-                proj_ref[part(to, k), :], all_grad[...], preferred_element_type=jnp.float32
+                proj_v[part(to, k), :], all_grad[...], preferred_element_type=jnp.float32
             )
             part_grad[part(to, k), :] = got.astype(jnp.bfloat16)
             side = 0 if copies is first else 1
@@ -422,7 +465,7 @@
     for k in range(pieces):
         at = pl.ds(k * piece, piece)
         kept = jnp.dot(
-            proj_ref[part(mirror, k), :], all_grad[...], preferred_element_type=jnp.float32
+            proj_v[part(mirror, k), :], all_grad[...], preferred_element_type=jnp.float32
         )
         first[k].wait_recv()
         kept = kept + pair_grad[0, at, :].astype(jnp.float32)
@@ -431,7 +474,7 @@
     placed = []
     for k in range(pieces):
         at = pl.ds(k * piece, piece)
-        kept = jnp.dot(proj_ref[part(h, k), :], all_grad[...], preferred_element_type=jnp.float32)
+        kept = jnp.dot(proj_v[part(h, k), :], all_grad[...], preferred_element_type=jnp.float32)
         second[k].wait_recv()
         kept = kept + pair_grad[1, at, :].astype(jnp.float32)
         mirrored[k].wait_recv()
@@ -472,11 +515,13 @@
     rows, span = activations.shape
     channels = long_filters.shape[0]
     own = channels // ns
+    taps = medium_taps.shape[1]
     length = span * ns
     quarter = rows // nc
     pieces = 2
     copies = 9 * pieces + 3 * pieces + 3 * pieces + 6 * pieces + 24 + 16
     vmem = pl.BlockSpec(memory_space=pltpu.VMEM)
+    hbm = pl.BlockSpec(memory_space=pltpu.HBM)
     bf16 = jnp.bfloat16
     return pl.pallas_call(
         functools.partial(fused_kernel, ns, nc, pieces),
@@ -484,7 +529,7 @@
             jax.ShapeDtypeStruct((channels, span), bf16),
             jax.ShapeDtypeStruct((rows, span), bf16),
         ),
-        in_specs=[vmem] * 6,
+        in_specs=[hbm] * 6,
         out_specs=(vmem, vmem),
         scratch_shapes=[
             pltpu.VMEM((nc, quarter, span), bf16),
@@ -502,8 +547,13 @@
             pltpu.VMEM((quarter, length), bf16),
             pltpu.VMEM((ns, quarter, span), bf16),
             pltpu.VMEM((rows, span), bf16),
+            pltpu.VMEM((rows, channels), bf16),
+            pltpu.VMEM((channels, rows), bf16),
+            pltpu.VMEM((own, taps), jnp.float32),
+            pltpu.VMEM((length, 2 * length), bf16),
             pltpu.SemaphoreType.DMA((copies,)),
             pltpu.SemaphoreType.DMA((copies,)),
+            pltpu.SemaphoreType.DMA((8,)),
         ],
         compiler_params=pltpu.CompilerParams(
             collective_id=0, has_side_effects=True, vmem_limit_bytes=48 * 1024 * 1024

time: 79.2 us -> 75.8 us (0.957)
  Pallas kernels: 70.7 us -> 67.4 us
    pallas_call x1, Pallas kernels: 70.7 us -> 67.4 us  [fused_on_device(): pl.pallas_call(functools.partial(fused_kernel, ns, nc, pieces), out_shape...]
where the time goes in v2:
time: 75.8 us; the launch traced here: 75.5 us
  Pallas kernels  67.4 us (89%)
  local copies, waits for them, and re-layouts  7.51 us (10%)
    pallas_call x1, Pallas kernels, fused_on_device(): pl.pallas_call(functools.partial(fused_kernel, ns, nc, pieces), out_shape...  67.4 us
    unnamed x14, local copies, waits for them, and re-layouts  7.51 us

profile of v2, /device:TPU:0, one launch (start us, length us, event | category | flops | bytes accessed | tf_op | source)
XLA Modules:
  0.0 75.5 jit_solution(195619964270903587)
XLA Ops:
  0.6 0.0 copy-start
  0.6 1.2 %copy-done = bf16[1024,512]{1,0:T(8,128)(2,1)S(1)} copy-done((bf16[1024,512]{1,0:T(8,128)(2,1)S(1)}, bf16[1024,512]{1,0:T(8,128)(2,1)}, u32[]{:S(2)}) %copy-start) | copy-done | bytes 1048600
  1.9 0.0 copy-start.1
  1.9 1.2 %copy-done.1 = bf16[512,1024]{1,0:T(8,128)(2,1)S(1)} copy-done((bf16[512,1024]{1,0:T(8,128)(2,1)S(1)}, bf16[512,1024]{1,0:T(8,128)(2,1)}, u32[]{:S(2)}) %copy-start.1) | copy-done | bytes 1048600
  3.1 0.0 copy-start.2
  3.1 0.9 %copy-done.2 = bf16[1024,128]{1,0:T(8,128)(2,1)S(1)} copy-done((bf16[1024,128]{1,0:T(8,128)(2,1)S(1)}, bf16[1024,128]{1,0:T(8,128)(2,1)}, u32[]{:S(2)}) %copy-start.2) | copy-done | bytes 262168
  4.0 0.0 copy-start.3
  4.0 0.9 %copy-done.3 = f32[512,128]{1,0:T(8,128)S(1)} copy-done((f32[512,128]{1,0:T(8,128)S(1)}, f32[512,128]{1,0:T(8,128)}, u32[]{:S(2)}) %copy-start.3) | copy-done | bytes 262168
  5.0 0.0 copy-start.4
  5.0 0.9 %copy-done.4 = bf16[512,128]{1,0:T(8,128)(2,1)S(1)} copy-done((bf16[512,128]{1,0:T(8,128)(2,1)S(1)}, bf16[512,128]{1,0:T(8,128)(2,1)}, u32[]{:S(2)}) %copy-start.4) | copy-done | bytes 131096
  5.9 0.0 copy-start.5
  5.9 0.9 %copy-done.5 = bf16[512,128]{1,0:T(8,128)(2,1)S(1)} copy-done((bf16[512,128]{1,0:T(8,128)(2,1)S(1)}, bf16[512,128]{1,0:T(8,128)(2,1)}, u32[]{:S(2)}) %copy-start.5) | copy-done | bytes 131096
  6.8 67.4 %shard_map.77 = (bf16[512,128]{1,0:T(8,128)(2,1)S(1)}, bf16[1024,128]{1,0:T(8,128)(2,1)S(1)}) custom-call(bf16[1024,128]{1,0:T(8,128)(2,1)S(1)} %copy-done.2, bf16[1024,512]{1,0:T(8,128)(2,1)S(1)} %copy-done, f32[512,128]{1,0:T(8,128)S(1)} %copy-done.3, bf16[512,128]{1,0:T(8,128)(2,1)S(1)} %copy-done.4, bf16[512,128]{1,0:T(8,128)(2,1)S(1)} %copy-done.5, ...), custom_call_target="tpu_custom_call" | custom-call | tf_op jit(solution)/shard_map/pallas_call | solution.py:526
  74.2 0.7 copy.10
  74.8 0.7 copy.11
Async XLA Ops:
  0.6 1.2 %copy-start = (bf16[1024,512]{1,0:T(8,128)(2,1)S(1)}, bf16[1024,512]{1,0:T(8,128)(2,1)}, u32[]{:S(2)}) copy-start(bf16[1024,512]{1,0:T(8,128)(2,1)} %proj_ref.1) | copy-start | bytes 3145732
  1.9 1.2 %copy-start.1 = (bf16[512,1024]{1,0:T(8,128)(2,1)S(1)}, bf16[512,1024]{1,0:T(8,128)(2,1)}, u32[]{:S(2)}) copy-start(bf16[512,1024]{1,0:T(8,128)(2,1)} %constant.2.clone.table_ref) | copy-start | bytes 3145732
  3.1 0.9 %copy-start.2 = (bf16[1024,128]{1,0:T(8,128)(2,1)S(1)}, bf16[1024,128]{1,0:T(8,128)(2,1)}, u32[]{:S(2)}) copy-start(bf16[1024,128]{1,0:T(8,128)(2,1)} %act_ref.1) | copy-start | bytes 786436
  4.0 0.9 %copy-start.3 = (f32[512,128]{1,0:T(8,128)S(1)}, f32[512,128]{1,0:T(8,128)}, u32[]{:S(2)}) copy-start(f32[512,128]{1,0:T(8,128)} %taps_ref.1) | copy-start | bytes 786436
  5.0 0.9 %copy-start.4 = (bf16[512,128]{1,0:T(8,128)(2,1)S(1)}, bf16[512,128]{1,0:T(8,128)(2,1)}, u32[]{:S(2)}) copy-start(bf16[512,128]{1,0:T(8,128)(2,1)} %filt_ref.1) | copy-start | bytes 393220
  5.9 0.9 %copy-start.5 = (bf16[512,128]{1,0:T(8,128)(2,1)S(1)}, bf16[512,128]{1,0:T(8,128)(2,1)}, u32[]{:S(2)}) copy-start(bf16[512,128]{1,0:T(8,128)(2,1)} %cot_ref.1) | copy-start | bytes 393220

commit v3 on v2

--- a/solution.py
+++ b/solution.py
@@ -402,7 +402,13 @@
     mixed = jnp.dot(
         proj_t[block(s, own), :], all_act[...], preferred_element_type=jnp.float32
     )
-    gathered, mediums, gates = [], [], []
+    def place(p):
+        return p % 2 * (ns // 2) + p // 2
+
+    def stage_of(t, i):
+        return block((t + 1 + i) % 2, length // 2)
+
+    gathered, mediums, gates = ([], []), [], []
     for c in range(2):
         at = slice(c * half, (c + 1) * half)
         summed = mixed[at]
@@ -420,13 +426,17 @@
         )
         both = from_spectrum(*both, table)
         medium, through = both[:half], both[half:]
-        all_grad[half_of(s, c), :] = (
-            through + back[at] * medium * gate * (1.0 - gate)
-        ).astype(jnp.bfloat16)
-        gathered += [
-            send(all_grad.at[half_of(s, c), :], all_grad.at[half_of(s, c), :], seq=(s + d) % ns)
-            for d in range(1, ns)
-        ]
+        grads = (through + back[at] * medium * gate * (1.0 - gate)).astype(jnp.bfloat16)
+        for p in range(ns):
+            all_grad[half_of(s, c), pl.ds(place(p) * span, span)] = grads[
+                :, p * span : (p + 1) * span
+            ]
+        for i in range(2):
+            for d in range(1, ns):
+                where = (half_of(s, c), stage_of((s + d) % ns, i))
+                gathered[i].append(
+                    send(all_grad.at[where], all_grad.at[where], seq=(s + d) % ns)
+                )
         mediums.append(medium)
         gates.append(gate)
     medium, gate = jnp.concatenate(mediums, axis=0), jnp.concatenate(gates, axis=0)
@@ -444,53 +454,61 @@
     ]
     conv_got[block(s, own), :] = conv_own[:, block(s, span)]
 
-    for copy in gathered:
-        copy.wait_recv()
-    first, second = [], []
-    for k in range(pieces):
-        for to, copies in ((across, first), (partner, second)):
-            got = jnp.dot(
-                proj_v[part(to, k), :], all_grad[...], preferred_element_type=jnp.float32
-            )
-            part_grad[part(to, k), :] = got.astype(jnp.bfloat16)
-            side = 0 if copies is first else 1
-            copies.append(
+    def partial(to, i):
+        return jnp.dot(
+            proj_v[block(to, quarter), :],
+            all_grad[:, stage_of(s, i)],
+            preferred_element_type=jnp.float32,
+        )
+
+    seconds, mirrored = [], []
+    for i in range(2):
+        lanes = stage_of(s, i)
+        for copy in gathered[i]:
+            copy.wait_recv()
+        pair = []
+        for side, to in enumerate((across, partner)):
+            part_grad[block(to, quarter), lanes] = partial(to, i).astype(jnp.bfloat16)
+            pair.append(
                 send(
-                    part_grad.at[part(to, k), :],
-                    pair_grad.at[side, pl.ds(k * piece, piece), :],
+                    part_grad.at[block(to, quarter), lanes],
+                    pair_grad.at[side, :, lanes],
                     ch=partner,
                 )
             )
-    mirrored = []
-    for k in range(pieces):
-        at = pl.ds(k * piece, piece)
-        kept = jnp.dot(
-            proj_v[part(mirror, k), :], all_grad[...], preferred_element_type=jnp.float32
-        )
-        first[k].wait_recv()
-        kept = kept + pair_grad[0, at, :].astype(jnp.float32)
-        mirror_send[at, :] = kept.astype(jnp.bfloat16)
-        mirrored.append(send(mirror_send.at[at, :], mirror_got.at[at, :], ch=mirror))
-    placed = []
-    for k in range(pieces):
-        at = pl.ds(k * piece, piece)
-        kept = jnp.dot(proj_v[part(h, k), :], all_grad[...], preferred_element_type=jnp.float32)
-        second[k].wait_recv()
-        kept = kept + pair_grad[1, at, :].astype(jnp.float32)
-        mirrored[k].wait_recv()
-        kept = kept + mirror_got[at, :].astype(jnp.float32)
-        total_grad[at, :] = kept.astype(jnp.bfloat16)
-        placed.append(
-            [
-                send(
-                    total_grad.at[at, block((s + d) % ns, span)],
-                    turned.at[s, at, :],
-                    seq=(s + d) % ns,
-                )
-                for d in range(1, ns)
-            ]
-        )
-        turned[s, at, :] = total_grad[at, block(s, span)]
+        kept = partial(mirror, i)
+        pair[0].wait_recv()
+        kept = kept + pair_grad[0, :, lanes].astype(jnp.float32)
+        mirror_send[:, lanes] = kept.astype(jnp.bfloat16)
+        copies = []
+        for k in range(pieces):
+            at = pl.ds(k * piece, piece)
+            copies.append(send(mirror_send.at[at, lanes], mirror_got.at[at, lanes], ch=mirror))
+        seconds.append(pair[1])
+        mirrored.append(copies)
+    placed = [[] for _ in range(pieces)]
+    for i in range(2):
+        lanes = stage_of(s, i)
+        kept = partial(h, i)
+        seconds[i].wait_recv()
+        for k in range(pieces):
+            at = pl.ds(k * piece, piece)
+            some = kept[k * piece : (k + 1) * piece] + pair_grad[1, at, lanes].astype(jnp.float32)
+            mirrored[i][k].wait_recv()
+            some = some + mirror_got[at, lanes].astype(jnp.float32)
+            total_grad[at, lanes] = some.astype(jnp.bfloat16)
+            for d in range(1, ns):
+                if (d + 1 + i) % 2 == 0:
+                    to = (s + d) % ns
+                    placed[k].append(
+                        send(
+                            total_grad.at[at, block(place(to), span)],
+                            turned.at[s, at, :],
+                            seq=to,
+                        )
+                    )
+            if i == 1:
+                turned[s, at, :] = total_grad[at, block(place(s), span)]
     final = []
     for k in range(pieces):
         at = pl.ds(k * piece, piece)
@@ -556,7 +574,7 @@
             pltpu.SemaphoreType.DMA((8,)),
         ],
         compiler_params=pltpu.CompilerParams(
-            collective_id=0, has_side_effects=True, vmem_limit_bytes=48 * 1024 * 1024
+            collective_id=0, has_side_effects=True, vmem_limit_bytes=60 * 1024 * 1024
         ),
     )(activations, projection, medium_taps, long_filters, cotangent, transform_table(length))
 

time: 75.8 us -> 69.6 us (0.918)
  local copies, waits for them, and re-layouts: 7.51 us -> 2.32 us
  Pallas kernels: 67.4 us -> 66.5 us
    unnamed x14 -> x4, local copies, waits for them, and re-layouts: 7.51 us -> 2.32 us
    pallas_call x1, Pallas kernels: 67.4 us -> 66.5 us  [fused_on_device(): pl.pallas_call(functools.partial(fused_kernel, ns, nc, pieces), out_shape...]
where the time goes in v3:
time: 69.6 us; the launch traced here: 69.5 us
  Pallas kernels  66.5 us (96%)
  local copies, waits for them, and re-layouts  2.32 us (3%)
    pallas_call x1, Pallas kernels, fused_on_device(): pl.pallas_call(functools.partial(fused_kernel, ns, nc, pieces), out_shape...  66.5 us
    unnamed x4, local copies, waits for them, and re-layouts  2.32 us

profile of v3, /device:TPU:0, one launch (start us, length us, event | category | flops | bytes accessed | tf_op | source)
XLA Modules:
  0.0 69.5 jit_solution(15817384734030852043)
XLA Ops:
  0.6 66.5 %shard_map.77 = (bf16[512,128]{1,0:T(8,128)(2,1)}, bf16[1024,128]{1,0:T(8,128)(2,1)}) custom-call(bf16[1024,128]{1,0:T(8,128)(2,1)} %act_ref.1, bf16[1024,512]{1,0:T(8,128)(2,1)} %proj_ref.1, f32[512,128]{1,0:T(8,128)} %taps_ref.1, bf16[512,128]{1,0:T(8,128)(2,1)} %filt_ref.1, bf16[512,128]{1,0:T(8,128)(2,1)} %cot_ref.1, ...), custom_call_target="tpu_custom_call" | custom-call | tf_op jit(solution)/shard_map/pallas_call | solution.py:544
  67.1 0.0 copy-start
  67.2 1.6 %copy.10 = bf16[512,128]{1,0:T(8,128)(2,1)} copy(bf16[512,128]{1,0:T(8,128)(2,1)} %get-tuple-element.4) | data formatting | bytes 262144
  68.8 0.0 copy-done
  68.8 0.7 %copy.11 = bf16[1024,128]{1,0:T(8,128)(2,1)} copy(bf16[1024,128]{1,0:T(8,128)(2,1)S(1)} %copy-done) | data formatting | bytes 524288
Async XLA Ops:
  67.1 1.6 %copy-start = (bf16[1024,128]{1,0:T(8,128)(2,1)S(1)}, bf16[1024,128]{1,0:T(8,128)(2,1)}, u32[]{:S(2)}) copy-start(bf16[1024,128]{1,0:T(8,128)(2,1)} %get-tuple-element.5) | copy-start | bytes 786436

commit v4 on v3

--- a/solution.py
+++ b/solution.py
@@ -227,6 +227,7 @@
     wide_in,
     part_sum,
     got_sum,
+    far_got,
     conv_own,
     conv_got,
     all_grad,
@@ -257,6 +258,15 @@
     mirror = (h + nc // 2) % nc
     across = (partner + nc // 2) % nc
     started, loads = [], []
+
+    @pl.when(s == 0)
+    def _():
+        got_sum[0] = jnp.zeros_like(got_sum[0])
+
+    @pl.when(s == ns - 1)
+    def _():
+        got_sum[ns - 2] = jnp.zeros_like(got_sum[ns - 2])
+
     half = own // 2
 
     def block(index, size):
@@ -265,18 +275,22 @@
     def part(index, k):
         return pl.ds(pl.multiple_of(index * quarter + k * piece, piece), piece)
 
-    def send(src, dst, **where):
+    def send(src, dst, when=None, into=None, **where):
         slot = len(started)
+        into = slot if into is None else into
         copy = pltpu.make_async_remote_copy(
             src_ref=src,
             dst_ref=dst,
             send_sem=send_sems.at[slot],
-            recv_sem=recv_sems.at[slot],
+            recv_sem=recv_sems.at[into],
             device_id=where,
             device_id_type=MESH,
         )
-        copy.start()
-        started.append(copy)
+        if when is None:
+            copy.start()
+        else:
+            pl.when(when)(lambda: copy.start())
+        started.append((copy, when))
         return copy
 
     def load(src, dst):
@@ -381,39 +395,88 @@
     def half_of(index, c):
         return pl.ds(pl.multiple_of(index * own + c * half, half), half)
 
+    inner = (s != 0) & (s != ns - 1)
+    near = {1: s != ns - 1, 2: (s == 0) | (s == ns - 1), 3: s != 0}
+    reduced, sum_slots, far = {}, {}, {}
+
     def sum_to(d, c):
-        return send(
-            part_sum.at[half_of((s + d) % ns, c), :],
-            got_sum.at[d - 1, pl.ds(c * half, half), :],
+        rows_to = half_of((s + d) % ns, c)
+        at = pl.ds(c * half, half)
+        if d != 2:
+            far[c] = send(
+                part_sum.at[rows_to, :],
+                far_got.at[at, :],
+                when=s == (ns - 1 if d == 1 else 0),
+                into=sum_slots.setdefault(("far", c), len(started)),
+                seq=ns - 2 if d == 1 else 1,
+            )
+        sum_slots[c, d] = len(started)
+        reduced[c, d] = send(
+            part_sum.at[rows_to, :],
+            got_sum.at[d - 1, at, :],
+            when=near[d],
             seq=(s + d) % ns,
         )
 
-    reduced = [[], []]
-    for d in range(1, ns):
+    for d in (3, 1, 2):
         got = jnp.dot(
             proj_t[block((s + d) % ns, own), :],
             all_act[...],
             preferred_element_type=jnp.float32,
         )
         part_sum[block((s + d) % ns, own), :] = got.astype(jnp.bfloat16)
-        reduced[0].append(sum_to(d, 0))
-    for d in range(1, ns):
-        reduced[1].append(sum_to(d, 1))
+        sum_to(d, 0)
+    for d in (3, 1, 2):
+        sum_to(d, 1)
     mixed = jnp.dot(
         proj_t[block(s, own), :], all_act[...], preferred_element_type=jnp.float32
     )
+    for c in range(2):
+        at = pl.ds(c * half, half)
+        rows_to = half_of((s + 2) % ns, c)
+
+        @pl.when(inner)
+        def _(c=c, at=at, rows_to=rows_to):
+            far[c].wait_recv()
+            joined = part_sum[rows_to, :].astype(jnp.float32) + far_got[at, :].astype(jnp.float32)
+            part_sum[rows_to, :] = joined.astype(jnp.bfloat16)
+
+        send(
+            part_sum.at[rows_to, :],
+            got_sum.at[1, at, :],
+            when=inner,
+            into=sum_slots[c, 2],
+            seq=(s + 2) % ns,
+        )
+
     def place(p):
         return p % 2 * (ns // 2) + p // 2
 
     def stage_of(t, i):
         return block((t + 1 + i) % 2, length // 2)
 
-    gathered, mediums, gates = ([], []), [], []
+    def relay(c):
+        for i in range(2):
+            gathered[c, i, 2].wait_recv()
+            where = (half_of((s + 2) % ns, c), stage_of(s, i))
+            for end, d in ((0, 1), (ns - 1, 3)):
+                send(
+                    all_grad.at[where],
+                    all_grad.at[where],
+                    when=s == (1 if end == 0 else ns - 2),
+                    into=slots[c, 1 - i, d],
+                    seq=end,
+                )
+
+    gathered, slots, mediums, gates = {}, {}, [], []
     for c in range(2):
         at = slice(c * half, (c + 1) * half)
         summed = mixed[at]
         for d in range(1, ns):
-            reduced[c][d - 1].wait_recv()
+            if d == 2:
+                reduced[c, d].wait_recv()
+            else:
+                pl.when(s != (0 if d == 1 else ns - 1))(reduced[c, d].wait_recv)
             summed = summed + got_sum[d - 1, pl.ds(c * half, half), :].astype(jnp.float32)
         values = summed.astype(jnp.bfloat16)
         gate = jax.nn.sigmoid(values.astype(jnp.float32))
@@ -431,16 +494,18 @@
             all_grad[half_of(s, c), pl.ds(place(p) * span, span)] = grads[
                 :, p * span : (p + 1) * span
             ]
-        for i in range(2):
-            for d in range(1, ns):
-                where = (half_of(s, c), stage_of((s + d) % ns, i))
-                gathered[i].append(
-                    send(all_grad.at[where], all_grad.at[where], seq=(s + d) % ns)
-                )
+        for i, d in [(0, 2), (1, 2), (0, 1), (0, 3), (1, 1), (1, 3)]:
+            where = (half_of(s, c), stage_of((s + d) % ns, i))
+            near = {1: s != ns - 1, 2: None, 3: s != 0}[d]
+            slots[c, i, d] = len(started)
+            gathered[c, i, d] = send(
+                all_grad.at[where], all_grad.at[where], when=near, seq=(s + d) % ns
+            )
         mediums.append(medium)
         gates.append(gate)
     medium, gate = jnp.concatenate(mediums, axis=0), jnp.concatenate(gates, axis=0)
 
+    relay(0)
     gated = (medium * gate).astype(jnp.bfloat16)
     conv = from_spectrum(*times(to_spectrum(gated, table), filt), table)
     conv_own[...] = conv.astype(jnp.bfloat16)
@@ -454,6 +519,7 @@
     ]
     conv_got[block(s, own), :] = conv_own[:, block(s, span)]
 
+    relay(1)
     def partial(to, i):
         return jnp.dot(
             proj_v[block(to, quarter), :],
@@ -464,8 +530,8 @@
     seconds, mirrored = [], []
     for i in range(2):
         lanes = stage_of(s, i)
-        for copy in gathered[i]:
-            copy.wait_recv()
+        for c, d in ((0, 1), (0, 3), (1, 1), (1, 3)):
+            gathered[c, i, d].wait_recv()
         pair = []
         for side, to in enumerate((across, partner)):
             part_grad[block(to, quarter), lanes] = partial(to, i).astype(jnp.bfloat16)
@@ -525,8 +591,11 @@
     for copy in final:
         copy.wait_recv()
     grad_ref[...] = grad_got[...]
-    for copy in started:
-        copy.wait_send()
+    for copy, when in started:
+        if when is None:
+            copy.wait_send()
+        else:
+            pl.when(when)(lambda copy=copy: copy.wait_send())
 
 
 def fused_on_device(ns, nc, activations, projection, medium_taps, long_filters, cotangent):
@@ -537,7 +606,7 @@
     length = span * ns
     quarter = rows // nc
     pieces = 2
-    copies = 9 * pieces + 3 * pieces + 3 * pieces + 6 * pieces + 24 + 16
+    copies = 9 * pieces + 3 * pieces + 3 * pieces + 6 * pieces + 24 + 40
     vmem = pl.BlockSpec(memory_space=pltpu.VMEM)
     hbm = pl.BlockSpec(memory_space=pltpu.HBM)
     bf16 = jnp.bfloat16
@@ -555,6 +624,7 @@
             pltpu.VMEM((2 * own, length), bf16),
             pltpu.VMEM((channels, length), bf16),
             pltpu.VMEM((ns - 1, own, length), bf16),
+            pltpu.VMEM((own, length), bf16),
             pltpu.VMEM((own, length), bf16),
             pltpu.VMEM((channels, span), bf16),
             pltpu.VMEM((channels, length), bf16),

time: 69.6 us -> 67.3 us (0.967)
  Pallas kernels: 66.5 us -> 64.2 us
    pallas_call x1, Pallas kernels: 66.5 us -> 64.2 us  [fused_on_device(): pl.pallas_call(functools.partial(fused_kernel, ns, nc, pieces), out_shape...]
where the time goes in v4:
time: 67.3 us; the launch traced here: 67.1 us
  Pallas kernels  64.2 us (95%)
  local copies, waits for them, and re-layouts  2.32 us (3%)
    pallas_call x1, Pallas kernels, fused_on_device(): pl.pallas_call(functools.partial(fused_kernel, ns, nc, pieces), out_shape...  64.2 us
    unnamed x4, local copies, waits for them, and re-layouts  2.32 us

profile of v4, /device:TPU:0, one launch (start us, length us, event | category | flops | bytes accessed | tf_op | source)
XLA Modules:
  0.0 67.1 jit_solution(5307177940435598945)
XLA Ops:
  0.6 64.2 %shard_map.77 = (bf16[512,128]{1,0:T(8,128)(2,1)}, bf16[1024,128]{1,0:T(8,128)(2,1)}) custom-call(bf16[1024,128]{1,0:T(8,128)(2,1)} %act_ref.1, bf16[1024,512]{1,0:T(8,128)(2,1)} %proj_ref.1, f32[512,128]{1,0:T(8,128)} %taps_ref.1, bf16[512,128]{1,0:T(8,128)(2,1)} %filt_ref.1, bf16[512,128]{1,0:T(8,128)(2,1)} %cot_ref.1, ...), custom_call_target="tpu_custom_call" | custom-call | tf_op jit(solution)/shard_map/pallas_call | solution.py:613
  64.8 0.0 copy-start
  64.8 1.6 %copy.10 = bf16[512,128]{1,0:T(8,128)(2,1)} copy(bf16[512,128]{1,0:T(8,128)(2,1)} %get-tuple-element.4) | data formatting | bytes 262144
  66.4 0.0 copy-done
  66.4 0.7 %copy.11 = bf16[1024,128]{1,0:T(8,128)(2,1)} copy(bf16[1024,128]{1,0:T(8,128)(2,1)S(1)} %copy-done) | data formatting | bytes 524288
Async XLA Ops:
  64.8 1.6 %copy-start = (bf16[1024,128]{1,0:T(8,128)(2,1)S(1)}, bf16[1024,128]{1,0:T(8,128)(2,1)}, u32[]{:S(2)}) copy-start(bf16[1024,128]{1,0:T(8,128)(2,1)} %get-tuple-element.5) | copy-start | bytes 786436

commit v5 on v4

--- a/solution.py
+++ b/solution.py
@@ -229,7 +229,6 @@
     got_sum,
     far_got,
     conv_own,
-    conv_got,
     all_grad,
     part_grad,
     pair_grad,
@@ -237,7 +236,6 @@
     mirror_got,
     total_grad,
     turned,
-    grad_got,
     proj_v,
     proj_t,
     taps_v,
@@ -367,23 +365,6 @@
         copy.wait()
     for at in range(ns):
         proj_t[pl.ds(at * own, own), :] = proj_v[:, pl.ds(at * own, own)].T
-    for copy in wide_own:
-        copy.wait()
-    for copy in wide:
-        copy.wait_recv()
-    table = table_v[...]
-    spec = to_spectrum(wide_in[...], table)
-    filt = (spec[0][:own], spec[1][:own])
-    cot = (spec[0][own:], spec[1][own:])
-    taps_own = taps_v[...]
-    taps_high = taps_own.astype(jnp.bfloat16)
-    taps_low = (taps_own - taps_high.astype(jnp.float32)).astype(jnp.bfloat16)
-    table_top = table_v[pl.ds(0, taps_own.shape[1]), :]
-    high = to_spectrum(taps_high, table_top)
-    low = to_spectrum(taps_low, table_top)
-    taps = (high[0] + low[0], high[1] + low[1])
-    back = from_spectrum(*times_conj(cot, filt), table).astype(jnp.bfloat16).astype(jnp.float32)
-
     for k in range(pieces):
         crossed[k].wait_recv()
         shared.append(
@@ -431,6 +412,23 @@
     mixed = jnp.dot(
         proj_t[block(s, own), :], all_act[...], preferred_element_type=jnp.float32
     )
+    for copy in wide_own:
+        copy.wait()
+    for copy in wide:
+        copy.wait_recv()
+    table = table_v[...]
+    spec = to_spectrum(wide_in[...], table)
+    filt = (spec[0][:own], spec[1][:own])
+    cot = (spec[0][own:], spec[1][own:])
+    taps_own = taps_v[...]
+    taps_high = taps_own.astype(jnp.bfloat16)
+    taps_low = (taps_own - taps_high.astype(jnp.float32)).astype(jnp.bfloat16)
+    table_top = table_v[pl.ds(0, taps_own.shape[1]), :]
+    high = to_spectrum(taps_high, table_top)
+    low = to_spectrum(taps_low, table_top)
+    taps = (high[0] + low[0], high[1] + low[1])
+    back = from_spectrum(*times_conj(cot, filt), table).astype(jnp.bfloat16).astype(jnp.float32)
+
     for c in range(2):
         at = pl.ds(c * half, half)
         rows_to = half_of((s + 2) % ns, c)
@@ -509,17 +507,17 @@
     gated = (medium * gate).astype(jnp.bfloat16)
     conv = from_spectrum(*times(to_spectrum(gated, table), filt), table)
     conv_own[...] = conv.astype(jnp.bfloat16)
+    relay(1)
     returned = [
         send(
             conv_own.at[:, block((s + d) % ns, span)],
-            conv_got.at[block(s, own), :],
+            conv_ref.at[block(s, own), :],
             seq=(s + d) % ns,
         )
         for d in range(1, ns)
     ]
-    conv_got[block(s, own), :] = conv_own[:, block(s, span)]
-
-    relay(1)
+    kept_out = [load(conv_own.at[:, block(s, span)], conv_ref.at[block(s, own), :])]
+
     def partial(to, i):
         return jnp.dot(
             proj_v[block(to, quarter), :],
@@ -581,16 +579,16 @@
         for copy in placed[k]:
             copy.wait_recv()
         final += [
-            send(turned.at[(h + d) % nc, at, :], grad_got.at[part(h, k), :], ch=(h + d) % nc)
+            send(turned.at[(h + d) % nc, at, :], grad_ref.at[part(h, k), :], ch=(h + d) % nc)
             for d in range(1, nc)
         ]
-        grad_got[part(h, k), :] = turned[h, at, :]
+        kept_out.append(load(turned.at[h, at, :], grad_ref.at[part(h, k), :]))
     for copy in returned:
         copy.wait_recv()
-    conv_ref[...] = conv_got[...]
     for copy in final:
         copy.wait_recv()
-    grad_ref[...] = grad_got[...]
+    for copy in kept_out:
+        copy.wait()
     for copy, when in started:
         if when is None:
             copy.wait_send()
@@ -607,7 +605,6 @@
     quarter = rows // nc
     pieces = 2
     copies = 9 * pieces + 3 * pieces + 3 * pieces + 6 * pieces + 24 + 40
-    vmem = pl.BlockSpec(memory_space=pltpu.VMEM)
     hbm = pl.BlockSpec(memory_space=pltpu.HBM)
     bf16 = jnp.bfloat16
     return pl.pallas_call(
@@ -617,7 +614,7 @@
             jax.ShapeDtypeStruct((rows, span), bf16),
         ),
         in_specs=[hbm] * 6,
-        out_specs=(vmem, vmem),
+        out_specs=(hbm, hbm),
         scratch_shapes=[
             pltpu.VMEM((nc, quarter, span), bf16),
             pltpu.VMEM((rows, length), bf16),
@@ -626,7 +623,6 @@
             pltpu.VMEM((ns - 1, own, length), bf16),
             pltpu.VMEM((own, length), bf16),
             pltpu.VMEM((own, length), bf16),
-            pltpu.VMEM((channels, span), bf16),
             pltpu.VMEM((channels, length), bf16),
             pltpu.VMEM((rows, length), bf16),
             pltpu.VMEM((2, quarter, length), bf16),
@@ -634,14 +630,13 @@
             pltpu.VMEM((quarter, length), bf16),
             pltpu.VMEM((quarter, length), bf16),
             pltpu.VMEM((ns, quarter, span), bf16),
-            pltpu.VMEM((rows, span), bf16),
             pltpu.VMEM((rows, channels), bf16),
             pltpu.VMEM((channels, rows), bf16),
             pltpu.VMEM((own, taps), jnp.float32),
             pltpu.VMEM((length, 2 * length), bf16),
             pltpu.SemaphoreType.DMA((copies,)),
             pltpu.SemaphoreType.DMA((copies,)),
-            pltpu.SemaphoreType.DMA((8,)),
+            pltpu.SemaphoreType.DMA((16,)),
         ],
         compiler_params=pltpu.CompilerParams(
             collective_id=0, has_side_effects=True, vmem_limit_bytes=60 * 1024 * 1024

time: 67.3 us -> 63.8 us (0.948)
  Pallas kernels: 64.2 us -> 60.6 us
    pallas_call x1, Pallas kernels: 64.2 us -> 60.6 us  [fused_on_device(): pl.pallas_call(functools.partial(fused_kernel, ns, nc, pieces), out_shape...]
where the time goes in v5:
time: 63.8 us; the launch traced here: 63.5 us
  Pallas kernels  60.6 us (95%)
  local copies, waits for them, and re-layouts  2.32 us (4%)
  between operations  0.65 us (1%)
    pallas_call x1, Pallas kernels, fused_on_device(): pl.pallas_call(functools.partial(fused_kernel, ns, nc, pieces), out_shape...  60.6 us
    unnamed x4, local copies, waits for them, and re-layouts  2.32 us

profile of v5, /device:TPU:0, one launch (start us, length us, event | category | flops | bytes accessed | tf_op | source)
XLA Modules:
  0.0 63.5 jit_solution(4594827618640070373)
XLA Ops:
  0.6 60.6 %shard_map.77 = (bf16[512,128]{1,0:T(8,128)(2,1)}, bf16[1024,128]{1,0:T(8,128)(2,1)}) custom-call(bf16[1024,128]{1,0:T(8,128)(2,1)} %act_ref.1, bf16[1024,512]{1,0:T(8,128)(2,1)} %proj_ref.1, f32[512,128]{1,0:T(8,128)} %taps_ref.1, bf16[512,128]{1,0:T(8,128)(2,1)} %filt_ref.1, bf16[512,128]{1,0:T(8,128)(2,1)} %cot_ref.1, ...), custom_call_target="tpu_custom_call" | custom-call | tf_op jit(solution)/shard_map/pallas_call | solution.py:610
  61.2 0.0 copy-start
  61.2 1.6 %copy.10 = bf16[512,128]{1,0:T(8,128)(2,1)} copy(bf16[512,128]{1,0:T(8,128)(2,1)} %get-tuple-element.4) | data formatting | bytes 262144
  62.8 0.0 copy-done
  62.8 0.7 %copy.11 = bf16[1024,128]{1,0:T(8,128)(2,1)} copy(bf16[1024,128]{1,0:T(8,128)(2,1)S(1)} %copy-done) | data formatting | bytes 524288
Async XLA Ops:
  61.2 1.6 %copy-start = (bf16[1024,128]{1,0:T(8,128)(2,1)S(1)}, bf16[1024,128]{1,0:T(8,128)(2,1)}, u32[]{:S(2)}) copy-start(bf16[1024,128]{1,0:T(8,128)(2,1)} %get-tuple-element.5) | copy-start | bytes 786436

commit v6 on v5

--- a/solution.py
+++ b/solution.py
@@ -329,6 +329,19 @@
             ]
         )
     act_own.wait()
+    wide = []
+
+    def widen(at, ref):
+        for d in range(1, ns):
+            wide.append(
+                send(
+                    ref.at[block((s + d) % ns, own), :],
+                    wide_in.at[pl.ds(at * own, own), block(s, span)],
+                    seq=(s + d) % ns,
+                )
+            )
+
+    widen(0, filt_ref)
     moved = []
     for k in range(pieces):
         for copy in spread[k]:
@@ -344,16 +357,7 @@
             ]
         )
     all_act[block(h, quarter), block(s, span)] = held_act[s]
-    wide = []
-    for at, ref in enumerate((filt_ref, cot_ref)):
-        for d in range(1, ns):
-            wide.append(
-                send(
-                    ref.at[block((s + d) % ns, own), :],
-                    wide_in.at[pl.ds(at * own, own), block(s, span)],
-                    seq=(s + d) % ns,
-                )
-            )
+    widen(1, cot_ref)
     shared, crossed = [], []
     for k in range(pieces):
         for copy in moved[k]:

time: 63.8 us -> 63.8 us (level)
  no operation moved by 1% of the time
where the time goes in v6:
time: 63.8 us; the launch traced here: 63.6 us
  Pallas kernels  60.6 us (95%)
  local copies, waits for them, and re-layouts  2.32 us (4%)
  between operations  0.65 us (1%)
    pallas_call x1, Pallas kernels, fused_on_device(): pl.pallas_call(functools.partial(fused_kernel, ns, nc, pieces), out_shape...  60.6 us
    unnamed x4, local copies, waits for them, and re-layouts  2.32 us

profile of v6, /device:TPU:0, one launch (start us, length us, event | category | flops | bytes accessed | tf_op | source)
XLA Modules:
  0.0 63.6 jit_solution(8930553485274477414)
XLA Ops:
  0.6 60.6 %shard_map.77 = (bf16[512,128]{1,0:T(8,128)(2,1)}, bf16[1024,128]{1,0:T(8,128)(2,1)}) custom-call(bf16[1024,128]{1,0:T(8,128)(2,1)} %act_ref.1, bf16[1024,512]{1,0:T(8,128)(2,1)} %proj_ref.1, f32[512,128]{1,0:T(8,128)} %taps_ref.1, bf16[512,128]{1,0:T(8,128)(2,1)} %filt_ref.1, bf16[512,128]{1,0:T(8,128)(2,1)} %cot_ref.1, ...), custom_call_target="tpu_custom_call" | custom-call | tf_op jit(solution)/shard_map/pallas_call | solution.py:614
  61.3 0.0 copy-start
  61.3 1.6 %copy.10 = bf16[512,128]{1,0:T(8,128)(2,1)} copy(bf16[512,128]{1,0:T(8,128)(2,1)} %get-tuple-element.4) | data formatting | bytes 262144
  62.9 0.0 copy-done
  62.9 0.7 %copy.11 = bf16[1024,128]{1,0:T(8,128)(2,1)} copy(bf16[1024,128]{1,0:T(8,128)(2,1)S(1)} %copy-done) | data formatting | bytes 524288
Async XLA Ops:
  61.3 1.6 %copy-start = (bf16[1024,128]{1,0:T(8,128)(2,1)S(1)}, bf16[1024,128]{1,0:T(8,128)(2,1)}, u32[]{:S(2)}) copy-start(bf16[1024,128]{1,0:T(8,128)(2,1)} %get-tuple-element.5) | copy-start | bytes 786436
